TPU v7x, 32 devices: a whole 2x2x4 slice. The times are simulated.
32 devices in a mesh: expert: 8 (over z, y), replica: 4 (over x, core).
Axes of the slice: x: 2, y: 2, z: 4, core: 2. Of those that a mesh axis runs over, the one named last changes fastest.
Arguments:
- tokens: bfloat16 [2048, 2880], P(('expert', 'replica')), may hold values from -6 to 6
- expert_ids: int32 [2048, 4], P(('expert', 'replica')), may hold values from 0 to 7, all different within a row; in each aligned block of 64 rows (0 to 63, 64 to 127, ...) at most 48 rows name the same one
- gate_codes: int32 [2048, 4], P(('expert', 'replica')), may hold values from 1 to 65535
- w_gate: bfloat16 [8, 2880, 2880], P('expert', None, 'replica'), may hold values from -0.109375 to 0.109375
- w_up: bfloat16 [8, 2880, 2880], P('expert', None, 'replica'), may hold values from -0.109375 to 0.109375
- w_down: bfloat16 [8, 2880, 2880], P('expert', 'replica'), may hold values from -0.109375 to 0.109375
Outputs:
- mixed: bfloat16 [2048, 2880], P(('expert', 'replica'))
Inputs may be any that keep to these rules, and one draw needn't show every extreme that they name: `expert_ids`: each row names 4 different experts. Among the 64 rows of one device each expert is named at most 48 times, a bound that some block reaches.
All inputs are finite; a program needn't handle non-finite values.
Results may differ from a plain program's by a relative error of at most 0.015.
Values may be sent and summed in bfloat16 or wider, within the bound.
A program may use at most 128 MiB of HBM per device.

v0:
```python
import functools

import jax
import jax.numpy as jnp
from jax import lax
from jax.experimental import pallas as pl
from jax.experimental.pallas import tpu as pltpu
from jax.sharding import PartitionSpec as P

MESH = pl.DeviceIdType.MESH
CORES = 2
LANES = 128


def activate(gate, up):
    return gate * jax.nn.sigmoid(1.702 * gate) * (up + 1.0)


def spans(extent, step):
    return [(low, min(low + step, extent)) for low in range(0, extent, step)]


def fused(
    depth, experts, cap, tokens, meta, w_gate, w_up, w_down, out,
    tok_buf, meta_buf, y_out, x_buf, wg, wu, wd, hid, part, c_in, x_out, x_in,
    mine, y_in, z_out, z_in, acc, w_sem,
    zt_s, zt_r, zm_s, zm_r, y_s, y_r, xa_s, xa_r, xb_s, xb_r, c_s, c_r,
    pc_s, pc_r, pa_s, pa_r, pb_s, pb_r, py_s, py_r, pz_s, pz_r,
):
    rows, width = tokens.shape
    f32, bf16 = jnp.float32, jnp.bfloat16
    expert, replica = lax.axis_index("expert"), lax.axis_index("replica")
    z, y = expert // 2, expert % 2
    other = z * 2 + (1 - y)
    y_peer = {"expert": other}
    x_peer = {"replica": (replica + CORES) % (2 * CORES)}
    c_peer = {"replica": replica // CORES * CORES + (1 - replica % CORES)}

    def z_peer(back):
        return {"expert": ((z + depth - back) % depth) * 2 + y}

    def z_ahead(ahead):
        return {"expert": ((z + ahead) % depth) * 2 + y}

    def send(src, dst, ssem, rsem, peer):
        pltpu.make_async_remote_copy(
            src_ref=src, dst_ref=dst, send_sem=ssem, recv_sem=rsem,
            device_id=peer, device_id_type=MESH,
        ).start()

    def arrived(dst, sem):
        pltpu.make_async_copy(dst, dst, sem).wait()

    barrier = pltpu.get_barrier_semaphore()
    for peer in [z_peer(s) for s in range(1, depth)] + [y_peer, x_peer, c_peer]:
        pl.semaphore_signal(barrier, inc=1, device_id=peer, device_id_type=MESH)
    pl.semaphore_wait(barrier, depth + 2)

    for s in range(1, depth):
        send(meta, meta_buf.at[s], zm_s.at[s], zm_r.at[s], z_peer(s))
        send(tokens, tok_buf.at[s], zt_s.at[s], zt_r.at[s], z_peer(s))
    pltpu.make_async_copy(meta, meta_buf.at[0], zm_r.at[0]).start()
    pltpu.make_async_copy(tokens, tok_buf.at[0], zt_r.at[0]).start()
    loads = [
        pltpu.make_async_copy(src.at[0], dst, w_sem.at[i])
        for i, (src, dst) in enumerate(((w_gate, wg), (w_up, wu), (w_down, wd)))
    ]
    for load in loads:
        load.start()

    group = 2 * cap

    def pick(s, which):
        ranks = meta_buf[s, pl.ds(rows, 2 * experts), :]
        sub = lax.broadcasted_iota(jnp.int32, ranks.shape, 0)
        rank = jnp.sum(jnp.where(sub == which, ranks, 0.0), axis=0, keepdims=True)[:, :rows]
        slot = lax.broadcasted_iota(jnp.int32, (cap, rows), 0).astype(f32)
        return jnp.where(slot == rank, 1.0, 0.0).astype(bf16)

    def spread(s, which):
        ranks = meta_buf[s, pl.ds(0, rows), :]
        lane = lax.broadcasted_iota(jnp.int32, ranks.shape, 1)
        rank = jnp.sum(jnp.where(lane == which, ranks, 0.0), axis=1, keepdims=True)
        weight = jnp.sum(jnp.where(lane == which + experts, ranks, 0.0), axis=1, keepdims=True)
        slot = lax.broadcasted_iota(jnp.int32, (rows, cap), 1).astype(f32)
        return jnp.where(slot == rank, 1.0, 0.0).astype(bf16), weight

    def choose(s):
        arrived(meta_buf.at[s], zm_r.at[s])
        arrived(tok_buf.at[s], zt_r.at[s])
        block = tok_buf[s]
        y_out[s] = jnp.dot(pick(s, other), block, preferred_element_type=f32).astype(bf16)
        send(y_out.at[s], x_buf.at[s, pl.ds(cap, cap)], y_s.at[s], y_r.at[s], y_peer)
        x_buf[s, pl.ds(0, cap), :] = jnp.dot(
            pick(s, expert), block, preferred_element_type=f32
        ).astype(bf16)
        send(x_buf.at[s, pl.ds(0, cap)], x_buf.at[s, pl.ds(group, cap)],
             xa_s.at[s], xa_r.at[s], x_peer)

    def to_x(s):
        arrived(y_out.at[s], y_r.at[s])
        send(x_buf.at[s, pl.ds(cap, cap)], x_buf.at[s, pl.ds(group + cap, cap)],
             xb_s.at[s], xb_r.at[s], x_peer)

    def to_core(s):
        arrived(y_out.at[s], xa_r.at[s])
        arrived(y_out.at[s], xb_r.at[s])
        send(x_buf.at[s, pl.ds(0, 2 * group)], x_buf.at[s, pl.ds(2 * group, 2 * group)],
             c_s.at[s], c_r.at[s], c_peer)

    def ffn(s):
        arrived(c_in.at[s], c_r.at[s])

        @pl.when(s == 0)
        def _():
            for load in loads:
                load.wait()

        across = (((1,), (1,)), ((), ()))
        for low, high in spans(wg.shape[0], 256):
            block = x_buf[s]
            gate = lax.dot_general(block, wg[low:high, :], across, preferred_element_type=f32)
            up = lax.dot_general(block, wu[low:high, :], across, preferred_element_type=f32)
            hid[:, low:high] = activate(gate, up).astype(bf16)
        for low, high in spans(width, 512):
            part[s, :, low:high] = jnp.dot(
                hid[...], wd[:, low:high], preferred_element_type=f32
            ).astype(bf16)
        send(part.at[s, pl.ds(2 * group, 2 * group)], c_in.at[s], pc_s.at[s], pc_r.at[s], c_peer)

    def turn(i):
        return (i + 1) % depth

    def sum_core(i):
        s = turn(i)
        arrived(c_in.at[s], pc_r.at[s])
        for low, ssem, rsem in ((cap, pa_s, pa_r), (0, pb_s, pb_r)):
            x_out[s, pl.ds(low, cap), :] = (
                part[s, pl.ds(group + low, cap), :].astype(f32)
                + c_in[s, pl.ds(group + low, cap), :].astype(f32)
            ).astype(bf16)
            send(x_out.at[s, pl.ds(low, cap)], x_in.at[s, pl.ds(low, cap)],
                 ssem.at[s], rsem.at[s], x_peer)

    def add_up(s, low, rsem):
        arrived(y_in.at[s], rsem.at[s])
        mine[s, pl.ds(low, cap), :] = (
            part[s, pl.ds(low, cap), :].astype(f32)
            + c_in[s, pl.ds(low, cap), :].astype(f32)
            + x_in[s, pl.ds(low, cap), :].astype(f32)
        ).astype(bf16)

    def sum_x(i):
        s = turn(i)
        add_up(s, cap, pa_r)
        send(mine.at[s, pl.ds(cap, cap)], y_in.at[s], py_s.at[s], py_r.at[s], y_peer)
        add_up(s, 0, pb_r)

    def combine(i):
        s = turn(i)
        arrived(y_in.at[s], py_r.at[s])
        own_spread, own_weight = spread(s, expert)
        far_spread, far_weight = spread(s, other)
        total = own_weight * jnp.dot(
            own_spread, mine[s, pl.ds(0, cap), :], preferred_element_type=f32
        ) + far_weight * jnp.dot(far_spread, y_in[s], preferred_element_type=f32)

        @pl.when(s == 0)
        def _():
            acc[...] = total

        @pl.when(s > 0)
        def _():
            z_out[s] = total.astype(bf16)
            send(z_out.at[s], z_in.at[s], pz_s.at[s], pz_r.at[s], z_ahead(s))

    steps = ((choose, 0), (to_core, 1), (to_x, 0), (sum_core, 4), (ffn, 2), (sum_x, 5), (combine, 6))

    def tick(t, carry):
        for step, lag in steps:
            @pl.when((t >= lag) & (t < depth + lag))
            def _():
                step(t - lag)
        return carry

    lax.fori_loop(0, depth + steps[-1][1], tick, 0)

    total = acc[...]
    for s in range(1, depth):
        arrived(z_in.at[s], pz_r.at[s])
        total = total + z_in[s].astype(f32)
    out[...] = total.astype(bf16)
    for s in range(depth):
        if s:
            arrived(meta_buf.at[s], zm_s.at[s])
            arrived(tok_buf.at[s], zt_s.at[s])
            arrived(z_out.at[s], pz_s.at[s])
        arrived(y_out.at[s], y_s.at[s])
        arrived(c_in.at[s], c_s.at[s])
        arrived(c_in.at[s], pc_s.at[s])
        for sem in (xa_s, xb_s, pa_s, pb_s, py_s):
            arrived(y_in.at[s], sem.at[s])


def gathered_plan(tokens, expert_ids, gate_codes, w_gate, w_up, w_down, capacity, expert_count):
    rows, top = expert_ids.shape
    width = tokens.shape[1]
    w_gate, w_up = jnp.swapaxes(w_gate, 1, 2), jnp.swapaxes(w_up, 1, 2)
    part_width = w_gate.shape[1]
    depth = lax.axis_size("expert") // 2
    f32, bf16 = jnp.float32, jnp.bfloat16
    onehot = expert_ids[:, :, None] == jnp.arange(expert_count, dtype=jnp.int32)
    named = jnp.sum(onehot.astype(f32), axis=1)
    weights = jnp.sum(
        jnp.where(onehot, (gate_codes.astype(f32) / 65536.0)[:, :, None], 0.0), axis=1
    )
    before = jnp.arange(rows)[:, None] >= jnp.arange(rows)[None, :]
    counts = jnp.sum(jnp.where(before[:, :, None], named[None, :, :], 0.0), axis=1)
    ranks = jnp.where(named > 0, counts - 1.0, -1.0)
    table = jnp.concatenate([ranks, weights], axis=1)
    flat = jnp.pad(table, ((0, 0), (0, LANES - 2 * expert_count)))
    turned = jnp.pad(table.T, ((0, 0), (0, LANES - rows)))
    meta = jnp.concatenate([flat, turned], axis=0)
    group = 2 * capacity
    vm = pltpu.VMEM
    pairs = [pltpu.SemaphoreType.DMA((depth,))] * 22
    return pl.pallas_call(
        functools.partial(fused, depth, expert_count, capacity),
        out_shape=jax.ShapeDtypeStruct((rows, width), bf16),
        in_specs=[pl.BlockSpec(memory_space=pltpu.VMEM)] * 2
        + [pl.BlockSpec(memory_space=pl.ANY)] * 3,
        out_specs=pl.BlockSpec(memory_space=pltpu.VMEM),
        scratch_shapes=[
            vm((depth, rows, width), bf16),
            vm((depth,) + meta.shape, f32),
            vm((depth, capacity, width), bf16),
            vm((depth, 4 * group, width), bf16),
            vm(w_gate.shape[1:], bf16),
            vm(w_up.shape[1:], bf16),
            vm(w_down.shape[1:], bf16),
            vm((4 * group, part_width), bf16),
            vm((depth, 4 * group, width), bf16),
            vm((depth, 2 * group, width), bf16),
            vm((depth, group, width), bf16),
            vm((depth, group, width), bf16),
            vm((depth, group, width), bf16),
            vm((depth, capacity, width), bf16),
            vm((depth, rows, width), bf16),
            vm((depth, rows, width), bf16),
            vm((rows, width), f32),
            pltpu.SemaphoreType.DMA((3,)),
        ] + pairs,
        compiler_params=pltpu.CompilerParams(
            collective_id=0, has_side_effects=True, vmem_limit_bytes=63 << 20
        ),
    )(tokens, meta, w_gate, w_up, w_down)


def slot_plan(tokens, expert_ids, gate_codes, w_gate, w_up, w_down):
    tok_rows, top_count = expert_ids.shape
    width = tokens.shape[1]
    expert_count = lax.axis_size("expert") * w_gate.shape[0]
    capacity = 3 * tok_rows * top_count // (2 * expert_count)
    slot_count = expert_count * capacity
    flat_ids = expert_ids.reshape(-1)
    onehot = (flat_ids[:, None] == jnp.arange(expert_count, dtype=jnp.int32)[None, :]).astype(
        jnp.int32
    )
    ranking = jnp.sum((jnp.cumsum(onehot, axis=0) - 1) * onehot, axis=1)
    target = flat_ids * capacity + ranking
    picker = (target[:, None] == jnp.arange(slot_count, dtype=jnp.int32)[None, :]).astype(
        jnp.bfloat16
    )
    selector = jnp.sum(picker.reshape(tok_rows, top_count, slot_count), axis=1)
    outgoing = jnp.einsum("ts,td->sd", selector, tokens, preferred_element_type=jnp.float32).astype(
        jnp.bfloat16
    )
    arrived = lax.all_to_all(outgoing, "expert", split_axis=0, concat_axis=0, tiled=True)
    gathered = lax.all_gather(arrived, "replica", axis=0, tiled=True)
    gate = jnp.dot(gathered, w_gate[0], preferred_element_type=jnp.float32)
    up = jnp.dot(gathered, w_up[0], preferred_element_type=jnp.float32)
    hidden = activate(gate, up).astype(jnp.bfloat16)
    summed = lax.psum_scatter(
        jnp.dot(hidden, w_down[0], preferred_element_type=jnp.float32).astype(jnp.bfloat16),
        "replica",
        scatter_dimension=0,
        tiled=True,
    )
    returned = lax.all_to_all(summed, "expert", split_axis=0, concat_axis=0, tiled=True)
    per_choice = jnp.dot(picker, returned, preferred_element_type=jnp.float32)
    gates = gate_codes.astype(jnp.float32) / 65536.0
    weighted = per_choice.reshape(tok_rows, top_count, width) * gates[:, :, None]
    return jnp.sum(weighted, axis=1).astype(jnp.bfloat16)


def on_device(tokens, expert_ids, gate_codes, w_gate, w_up, w_down):
    rows, top = expert_ids.shape
    expert_count = lax.axis_size("expert") * w_gate.shape[0]
    capacity = 3 * rows * top // (2 * expert_count)
    args = (tokens, expert_ids, gate_codes, w_gate, w_up, w_down)
    paired = w_gate.shape[0] == 1 and lax.axis_size("replica") == 2 * CORES
    if paired and 2 * capacity > rows:
        return gathered_plan(*args, capacity, expert_count)
    return slot_plan(*args)


def solution(mesh):
    return jax.shard_map(
        on_device,
        mesh=mesh,
        in_specs=(
            P(("expert", "replica"), None),
            P(("expert", "replica"), None),
            P(("expert", "replica"), None),
            P("expert", None, "replica"),
            P("expert", None, "replica"),
            P("expert", "replica", None),
        ),
        out_specs=P(("expert", "replica"), None),
        check_vma=False,
    )
```

profile of v0, /device:TPU:0, one launch (start us, length us, event | category | flops | bytes accessed | tf_op | source)
XLA Modules:
  0.0 133.1 jit_solution(11099000638137261008)
XLA Ops:
  0.0 0.7 convert_multiply_fusion
  0.7 0.7 convert_reduce_fusion
  1.4 0.1 select_reduce_fusion
  1.5 0.1 copy.11
  1.6 0.1 copy.13
  1.7 0.6 select_maximum_fusion.meta
  2.3 129.0 %shard_map.64 = bf16[64,2880]{1,0:T(8,128)(2,1)} custom-call(bf16[64,2880]{1,0:T(8,128)(2,1)} %tokens.1, f32[80,128]{1,0:T(8,128)} %select_maximum_fusion.meta, bf16[1,720,2880]{2,1,0:T(8,128)(2,1)} %bitcast.4, bf16[1,720,2880]{2,1,0:T(8,128)(2,1)} %bitcast.5, bf16[1,720,2880]{2,1,0:T(8,128)(2,1)} %w_down.1), custom_call_target="tpu_custom_call" | custom-call | tf_op jit(solution)/shard_map/pallas_call | solution.py:227
  131.3 1.8 %copy.15 = bf16[64,2880]{1,0:T(8,128)(2,1)} copy(bf16[64,2880]{1,0:T(8,128)(2,1)} %shard_map.64) | data formatting | bytes 737280
  (3 shorter events, 0.0 us)
where the time goes:
time: 135 us; the launch traced here: 133 us
  Pallas kernels  129 us (96%)
  other arithmetic  2.18 us (2%)
  local copies, waits for them, and re-layouts  1.9 us (1%)
    pallas_call x1, Pallas kernels, gathered_plan(): pl.pallas_call(functools.partial(fused, depth, expert_count, capacity), o...  129 us

commit v1 on v0

v1 whole, which is shorter than its diff:
```python
import functools

import jax
import jax.numpy as jnp
from jax import lax
from jax.experimental import pallas as pl
from jax.experimental.pallas import tpu as pltpu
from jax.sharding import PartitionSpec as P

MESH = pl.DeviceIdType.MESH
CORES = 2


def activate(gate, up):
    return gate * jax.nn.sigmoid(1.702 * gate) * (up + 1.0)


def spans(extent, step):
    return [(low, min(low + step, extent)) for low in range(0, extent, step)]


def fused(
    depth, experts, cap, cut_in, cut_mid, cut_out, plan,
    tokens, ids, codes, w_gate, w_up, w_down, out,
    tok, far_tok, meta, far_meta, y_pick, x_buf, wg, wu, wd, hid, part, c_in,
    x_out, x_in, y_out, y_in, z_out, z_in, acc, w_sem,
    zt_s, zt_r, zf_s, zf_r, m_s, m_r, fm_s, fm_r, fx_s, raw_s, raw_r,
    ya_s, ya_r, yb_s, yb_r, xa_s, xa_r, xb_s, xb_r, c_s, c_r,
    pc_s, pc_r, pxa_s, pxa_r, pxb_s, pxb_r, pya_s, pya_r, pyb_s, pyb_r,
    pza_s, pza_r, pzb_s, pzb_r,
):
    rows, width = tokens.shape
    f32, bf16 = jnp.float32, jnp.bfloat16
    expert, replica = lax.axis_index("expert"), lax.axis_index("replica")
    z, y = expert // 2, expert % 2
    other = z * 2 + (1 - y)
    x_side = (replica + CORES) % (2 * CORES)
    y_peer = {"expert": other}
    x_peer = {"replica": x_side}
    c_peer = {"replica": replica // CORES * CORES + (1 - replica % CORES)}
    near, wide, rest = pl.ds(0, cut_in), pl.ds(cut_in, width - cut_in), pl.ds(cut_mid, width - cut_mid)
    mid = pl.ds(cut_in, cut_mid - cut_in)
    first, second = pl.ds(0, cut_out), pl.ds(cut_out, width - cut_out)
    group = 2 * cap

    def z_peer(level):
        return {"expert": level * 2 + y}

    def ahead(step):
        return (z + step) % depth

    def send(src, dst, ssem, rsem, peer):
        pltpu.make_async_remote_copy(
            src_ref=src, dst_ref=dst, send_sem=ssem, recv_sem=rsem,
            device_id=peer, device_id_type=MESH,
        ).start()

    def arrived(dst, sem):
        pltpu.make_async_copy(dst, dst, sem).wait()

    def block_at(i):
        pairs = jnp.minimum(z, depth - 1 - z)
        inward = jnp.where(2 * z < depth, 1, -1)
        beside = jnp.where(i % 2 == 1, z + inward * ((i + 1) // 2), z - inward * (i // 2))
        beyond = jnp.where(2 * z < depth, i, depth - 1 - i)
        return jnp.where(i <= 2 * pairs, beside, beyond)

    barrier = pltpu.get_barrier_semaphore()
    greeted = [y_peer, x_peer, c_peer]
    for step in range(1, depth):
        greeted.append(z_peer(ahead(step)))
    for peer in greeted:
        pl.semaphore_signal(barrier, inc=1, device_id=peer, device_id_type=MESH)
    own_load = pltpu.make_async_copy(tokens, tok.at[z], zt_r.at[z])
    own_load.start()
    loads = [
        pltpu.make_async_copy(src.at[0], dst, w_sem.at[i])
        for i, (src, dst) in enumerate(((w_gate, wg), (w_up, wu), (w_down, wd)))
    ]
    for load in loads:
        load.start()

    label = lax.broadcasted_iota(jnp.int32, (experts, rows), 0)
    named = jnp.zeros((experts, rows), f32)
    weight = jnp.zeros((experts, rows), f32)
    for k in range(ids.shape[0]):
        same = label == ids[k : k + 1, :]
        named = named + jnp.where(same, 1.0, 0.0)
        weight = weight + jnp.where(same, codes[k : k + 1, :].astype(f32) / 65536.0, 0.0)
    upto = lax.broadcasted_iota(jnp.int32, (rows, rows), 0) <= lax.broadcasted_iota(
        jnp.int32, (rows, rows), 1
    )
    counts = jnp.dot(
        named.astype(bf16), jnp.where(upto, 1.0, 0.0).astype(bf16), preferred_element_type=f32
    )
    meta[z, pl.ds(0, experts), :] = jnp.where(named > 0, counts - 1.0, -1.0)
    meta[z, pl.ds(experts, experts), :] = weight

    pl.semaphore_wait(barrier, len(greeted))
    own_load.wait()

    def pass_on(s, src, ssem, rsem):
        @pl.when((s <= z) & (z < depth - 1))
        def _():
            send(src, src, ssem.at[0, s], rsem.at[s], z_peer(ahead(1)))

        @pl.when((s >= z) & (z > 0))
        def _():
            send(src, src, ssem.at[1, s], rsem.at[s], z_peer(ahead(depth - 1)))

    def passed(s, src, ssem):
        @pl.when((s <= z) & (z < depth - 1))
        def _():
            arrived(src, ssem.at[0, s])

        @pl.when((s >= z) & (z > 0))
        def _():
            arrived(src, ssem.at[1, s])

    between = (z > 0) & (z < depth - 1)
    pass_on(z, meta.at[z], m_s, m_r)
    pass_on(z, tok.at[z], zt_s, zt_r)
    send(meta.at[z], far_meta.at[z], fx_s.at[0], fm_r.at[z], x_peer)
    send(tok.at[z, :, wide], far_tok.at[z, :, wide], raw_s.at[z], raw_r.at[z], x_peer)

    def row_of(table, which):
        sub = lax.broadcasted_iota(jnp.int32, table.shape, 0)
        return jnp.sum(jnp.where(sub == which, table, 0.0), axis=0, keepdims=True)

    def slots(table, which):
        slot = lax.broadcasted_iota(jnp.int32, (cap, rows), 0).astype(f32)
        return slot == row_of(table, which)

    def picker(table):
        return jnp.concatenate(
            [jnp.where(slots(table, e), 1.0, 0.0) for e in (expert, other)], axis=0
        ).astype(bf16)

    def spreader(table):
        high, low = [], []
        for e in (expert, other):
            share = row_of(table, e + experts)
            coarse = share.astype(bf16).astype(f32)
            here = slots(table, e)
            high.append(jnp.where(here, coarse, 0.0))
            low.append(jnp.where(here, share - coarse, 0.0))
        return jnp.concatenate(high + low, axis=0).astype(bf16)

    def spread(matrix, own, far):
        stacked = jnp.concatenate([own, far, own, far], axis=0)
        return lax.dot_general(
            matrix, stacked, (((0,), (0,)), ((), ())), preferred_element_type=f32
        )

    def relay(i):
        s = block_at(i)

        @pl.when(between)
        def _():
            arrived(meta.at[s], m_r.at[s])
            pass_on(s, meta.at[s], m_s, m_r)
            arrived(tok.at[s], zt_r.at[s])
            pass_on(s, tok.at[s], zt_s, zt_r)

    def relay_far(i):
        s = block_at(i)

        @pl.when(between)
        def _():
            arrived(far_meta.at[s], fm_r.at[s])
            pass_on(s, far_meta.at[s], fm_s, fm_r)
            if cut_mid < width:
                arrived(far_tok.at[s, :, rest], zf_r.at[s])
                pass_on(s, far_tok.at[s, :, rest], zf_s, zf_r)

    def choose(i):
        s = block_at(i)

        @pl.when((i > 0) & jnp.logical_not(between))
        def _():
            arrived(meta.at[s], m_r.at[s])
            arrived(tok.at[s], zt_r.at[s])

        if cut_mid > cut_in:
            @pl.when(i > 0)
            def _():
                send(tok.at[s, :, mid], far_tok.at[s, :, mid], raw_s.at[s], raw_r.at[s], x_peer)

        chosen = jnp.dot(picker(meta[s]), tok[s], preferred_element_type=f32).astype(bf16)
        x_buf[s, pl.ds(0, cap), :] = chosen[:cap]
        y_pick[s, pl.ds(0, cap), :] = chosen[cap:]
        send(y_pick.at[s, pl.ds(0, cap), near], x_buf.at[s, pl.ds(group, cap), near],
             ya_s.at[s], ya_r.at[s], y_peer)
        send(x_buf.at[s, pl.ds(0, cap), near], x_buf.at[s, pl.ds(cap, cap), near],
             xa_s.at[s], xa_r.at[s], x_peer)

    def choose_far(i):
        s = block_at(i)

        @pl.when(i == 0)
        def _():
            arrived(far_meta.at[s], fm_r.at[s])
            pass_on(s, far_meta.at[s], fm_s, fm_r)
            arrived(far_tok.at[s, :, wide], raw_r.at[s])
            if cut_mid < width:
                pass_on(s, far_tok.at[s, :, rest], zf_s, zf_r)

        @pl.when((i > 0) & jnp.logical_not(between))
        def _():
            arrived(far_meta.at[s], fm_r.at[s])
            if cut_mid < width:
                arrived(far_tok.at[s, :, rest], zf_r.at[s])

        if cut_mid > cut_in:
            @pl.when(i > 0)
            def _():
                arrived(far_tok.at[s, :, mid], raw_r.at[s])

        chosen = jnp.dot(
            picker(far_meta[s]), far_tok[s, :, wide], preferred_element_type=f32
        ).astype(bf16)
        x_buf[s, pl.ds(cap, cap), wide] = chosen[:cap]
        y_pick[s, pl.ds(cap, cap), wide] = chosen[cap:]
        send(y_pick.at[s, :, wide], x_buf.at[s, pl.ds(group, group), wide],
             yb_s.at[s], yb_r.at[s], y_peer)

    def forward(i):
        s = block_at(i)
        here = x_buf.at[s, pl.ds(group, cap), near]
        arrived(here, ya_r.at[s])
        send(here, x_buf.at[s, pl.ds(group + cap, cap), near], xb_s.at[s], xb_r.at[s], x_peer)

    def to_core(i):
        s = block_at(i)
        arrived(x_buf.at[s, pl.ds(cap, cap), near], xa_r.at[s])
        arrived(x_buf.at[s, pl.ds(group, group), wide], yb_r.at[s])
        arrived(x_buf.at[s, pl.ds(group + cap, cap), near], xb_r.at[s])
        send(x_buf.at[s, pl.ds(0, 2 * group)], x_buf.at[s, pl.ds(2 * group, 2 * group)],
             c_s.at[s], c_r.at[s], c_peer)

    def ffn_up(i):
        s = block_at(i)
        arrived(c_in.at[s], c_r.at[s])

        @pl.when(i == 0)
        def _():
            for load in loads:
                load.wait()

        across = (((1,), (1,)), ((), ()))
        for low, high in spans(wg.shape[0], 256):
            block = x_buf[s]
            gate = lax.dot_general(block, wg[low:high, :], across, preferred_element_type=f32)
            up = lax.dot_general(block, wu[low:high, :], across, preferred_element_type=f32)
            hid[:, low:high] = activate(gate, up).astype(bf16)

    def ffn_down(i):
        s = block_at(i)
        for low, high in spans(width, 512):
            part[s, :, low:high] = jnp.dot(
                hid[...], wd[:, low:high], preferred_element_type=f32
            ).astype(bf16)
        send(part.at[s, pl.ds(2 * group, 2 * group)], c_in.at[s], pc_s.at[s], pc_r.at[s], c_peer)

    def pair(s, low, count, cols):
        return part[s, pl.ds(low, count), cols].astype(f32) + c_in[s, pl.ds(low, count), cols].astype(f32)

    def sum_core(j):
        s = block_at(j)
        arrived(c_in.at[s], pc_r.at[s])
        for n in range(2):
            x_out[s, pl.ds(n * cap, cap), first] = pair(s, cap + n * group, cap, first).astype(bf16)
        send(x_out.at[s, :, first], x_in.at[s, :, first], pxa_s.at[s], pxa_r.at[s], x_peer)
        y_out[s, :, second] = pair(s, group, group, second).astype(bf16)
        send(y_out.at[s, :, second], y_in.at[s, :, second], pyb_s.at[s], pyb_r.at[s], y_peer)

    def sum_x(j):
        s = block_at(j)
        arrived(x_in.at[s, :, first], pxa_r.at[s])
        y_out[s, pl.ds(0, cap), first] = (
            pair(s, group, cap, first) + x_in[s, pl.ds(cap, cap), first].astype(f32)
        ).astype(bf16)
        send(y_out.at[s, pl.ds(0, cap), first], y_in.at[s, pl.ds(0, cap), first],
             pya_s.at[s], pya_r.at[s], y_peer)

    def sum_y(j):
        s = block_at(j)
        arrived(y_in.at[s, :, second], pyb_r.at[s])
        x_out[s, pl.ds(0, rows), second] = spread(
            spreader(far_meta[s]), pair(s, cap, cap, second).astype(bf16), y_in[s, pl.ds(cap, cap), second]
        ).astype(bf16)
        send(x_out.at[s, pl.ds(0, rows), second], x_in.at[s, pl.ds(0, rows), second],
             pxb_s.at[s], pxb_r.at[s], x_peer)

    def comb_a(j):
        s = block_at(j)
        arrived(y_in.at[s, pl.ds(0, cap), first], pya_r.at[s])
        own = (pair(s, 0, cap, first) + x_in[s, pl.ds(0, cap), first].astype(f32)).astype(bf16)
        total = spread(spreader(meta[s]), own, y_in[s, pl.ds(0, cap), first])

        @pl.when(s == z)
        def _():
            acc[:, first] = total

        @pl.when(s != z)
        def _():
            z_out[s, :, first] = total.astype(bf16)
            send(z_out.at[s, :, first], z_in.at[z, :, first], pza_s.at[s], pza_r.at[z], z_peer(s))

    def comb_b(j):
        s = block_at(j)
        arrived(x_in.at[s, pl.ds(0, rows), second], pxb_r.at[s])
        total = spread(
            spreader(meta[s]), pair(s, 0, cap, second).astype(bf16), y_in[s, pl.ds(0, cap), second]
        ) + x_in[s, pl.ds(0, rows), second].astype(f32)

        @pl.when(s == z)
        def _():
            acc[:, second] = total

        @pl.when(s != z)
        def _():
            z_out[s, :, second] = total.astype(bf16)
            send(z_out.at[s, :, second], z_in.at[z, :, second], pzb_s.at[s], pzb_r.at[z], z_peer(s))

    table = {
        "relay": relay, "relay_far": relay_far, "choose": choose, "choose_far": choose_far,
        "forward": forward, "to_core": to_core, "ffn_up": ffn_up, "ffn_down": ffn_down,
        "sum_core": sum_core, "sum_x": sum_x, "sum_y": sum_y, "comb_a": comb_a, "comb_b": comb_b,
    }

    def tick(t, carry):
        for name, starts in plan:
            hit, i = t < 0, 0
            for k, start in enumerate(starts):
                if start is not None:
                    hit = hit | (t == start)
                    i = jnp.where(t == start, k, i)

            @pl.when(hit)
            def _():
                table[name](i)
        return carry

    ticks = 1 + max(start for _, starts in plan for start in starts if start is not None)
    lax.fori_loop(0, ticks, tick, 0)

    total = acc[...]
    for step in range(1, depth):
        arrived(z_in.at[ahead(step), :, first], pza_r.at[ahead(step)])
        arrived(z_in.at[ahead(step), :, second], pzb_r.at[ahead(step)])
        total = total + z_in[ahead(step)].astype(f32)
    out[...] = total.astype(bf16)

    arrived(meta.at[0], fx_s.at[0])
    for s in range(depth):
        passed(s, meta.at[s], m_s)
        passed(s, tok.at[s], zt_s)
        passed(s, far_meta.at[s], fm_s)
        if cut_mid < width:
            passed(s, far_tok.at[s, :, rest], zf_s)

        @pl.when(s == z)
        def _():
            arrived(far_tok.at[s, :, wide], raw_s.at[s])

        @pl.when(s != z)
        def _():
            arrived(z_out.at[s, :, first], pza_s.at[s])
            arrived(z_out.at[s, :, second], pzb_s.at[s])
            if cut_mid > cut_in:
                arrived(far_tok.at[s, :, mid], raw_s.at[s])

        slab = x_buf.at[s, pl.ds(0, cap), near]
        for sem in (ya_s, xa_s, xb_s):
            arrived(slab, sem.at[s])
        arrived(y_pick.at[s, :, wide], yb_s.at[s])
        arrived(c_in.at[s], c_s.at[s])
        arrived(c_in.at[s], pc_s.at[s])
        arrived(x_out.at[s, :, first], pxa_s.at[s])
        arrived(y_out.at[s, pl.ds(0, cap), first], pya_s.at[s])
        arrived(y_out.at[s, :, second], pyb_s.at[s])
        arrived(x_out.at[s, pl.ds(0, rows), second], pxb_s.at[s])


CUTS = (1664, 2560, 1408)
PLAN = (
    ("ffn_down", (7, 8, 13, 12)),
    ("choose", (0, 3, 5, 7)),
    ("sum_x", (18, 12, 17, 13)),
    ("forward", (1, 3, 9, 8)),
    ("relay", (None, 1, 2, 5)),
    ("to_core", (3, 6, 12, 10)),
    ("sum_y", (17, 11, 16, 14)),
    ("sum_core", (16, 9, 14, 12)),
    ("comb_b", (18, 12, 16, 15)),
    ("comb_a", (18, 13, 17, 14)),
    ("ffn_up", (5, 7, 12, 10)),
    ("relay_far", (None, 4, 3, 7)),
    ("choose_far", (0, 4, 9, 7)),
)


def gathered_plan(tokens, expert_ids, gate_codes, w_gate, w_up, w_down, capacity, expert_count):
    rows, top = expert_ids.shape
    width = tokens.shape[1]
    w_gate, w_up = jnp.swapaxes(w_gate, 1, 2), jnp.swapaxes(w_up, 1, 2)
    part_width = w_gate.shape[1]
    depth = lax.axis_size("expert") // 2
    f32, bf16 = jnp.float32, jnp.bfloat16
    group = 2 * capacity
    vm, dma = pltpu.VMEM, pltpu.SemaphoreType.DMA
    one, two = dma((depth,)), dma((2, depth))
    return pl.pallas_call(
        functools.partial(fused, depth, expert_count, capacity, *CUTS, PLAN),
        out_shape=jax.ShapeDtypeStruct((rows, width), bf16),
        in_specs=[pl.BlockSpec(memory_space=pl.ANY)]
        + [pl.BlockSpec(memory_space=pltpu.VMEM)] * 2
        + [pl.BlockSpec(memory_space=pl.ANY)] * 3,
        out_specs=pl.BlockSpec(memory_space=pltpu.VMEM),
        scratch_shapes=[
            vm((depth, rows, width), bf16),
            vm((depth, rows, width), bf16),
            vm((depth, 2 * expert_count, rows), f32),
            vm((depth, 2 * expert_count, rows), f32),
            vm((depth, group, width), bf16),
            vm((depth, 4 * group, width), bf16),
            vm(w_gate.shape[1:], bf16),
            vm(w_up.shape[1:], bf16),
            vm(w_down.shape[1:], bf16),
            vm((4 * group, part_width), bf16),
            vm((depth, 4 * group, width), bf16),
            vm((depth, 2 * group, width), bf16),
            vm((depth, group, width), bf16),
            vm((depth, group, width), bf16),
            vm((depth, group, width), bf16),
            vm((depth, group, width), bf16),
            vm((depth, rows, width), bf16),
            vm((depth, rows, width), bf16),
            vm((rows, width), f32),
            dma((3,)),
        ]
        + [two, one] * 4
        + [dma((1,))]
        + [one] * 26,
        compiler_params=pltpu.CompilerParams(
            collective_id=0, has_side_effects=True, vmem_limit_bytes=63 << 20
        ),
    )(tokens, expert_ids.T, gate_codes.T, w_gate, w_up, w_down)


def slot_plan(tokens, expert_ids, gate_codes, w_gate, w_up, w_down):
    tok_rows, top_count = expert_ids.shape
    width = tokens.shape[1]
    expert_count = lax.axis_size("expert") * w_gate.shape[0]
    capacity = 3 * tok_rows * top_count // (2 * expert_count)
    slot_count = expert_count * capacity
    flat_ids = expert_ids.reshape(-1)
    onehot = (flat_ids[:, None] == jnp.arange(expert_count, dtype=jnp.int32)[None, :]).astype(
        jnp.int32
    )
    ranking = jnp.sum((jnp.cumsum(onehot, axis=0) - 1) * onehot, axis=1)
    target = flat_ids * capacity + ranking
    picker = (target[:, None] == jnp.arange(slot_count, dtype=jnp.int32)[None, :]).astype(
        jnp.bfloat16
    )
    selector = jnp.sum(picker.reshape(tok_rows, top_count, slot_count), axis=1)
    outgoing = jnp.einsum("ts,td->sd", selector, tokens, preferred_element_type=jnp.float32).astype(
        jnp.bfloat16
    )
    arrived = lax.all_to_all(outgoing, "expert", split_axis=0, concat_axis=0, tiled=True)
    gathered = lax.all_gather(arrived, "replica", axis=0, tiled=True)
    gate = jnp.dot(gathered, w_gate[0], preferred_element_type=jnp.float32)
    up = jnp.dot(gathered, w_up[0], preferred_element_type=jnp.float32)
    hidden = activate(gate, up).astype(jnp.bfloat16)
    summed = lax.psum_scatter(
        jnp.dot(hidden, w_down[0], preferred_element_type=jnp.float32).astype(jnp.bfloat16),
        "replica",
        scatter_dimension=0,
        tiled=True,
    )
    returned = lax.all_to_all(summed, "expert", split_axis=0, concat_axis=0, tiled=True)
    per_choice = jnp.dot(picker, returned, preferred_element_type=jnp.float32)
    gates = gate_codes.astype(jnp.float32) / 65536.0
    weighted = per_choice.reshape(tok_rows, top_count, width) * gates[:, :, None]
    return jnp.sum(weighted, axis=1).astype(jnp.bfloat16)


def on_device(tokens, expert_ids, gate_codes, w_gate, w_up, w_down):
    rows, top = expert_ids.shape
    expert_count = lax.axis_size("expert") * w_gate.shape[0]
    capacity = 3 * rows * top // (2 * expert_count)
    args = (tokens, expert_ids, gate_codes, w_gate, w_up, w_down)
    paired = w_gate.shape[0] == 1 and lax.axis_size("replica") == 2 * CORES
    if paired and 2 * capacity > rows:
        return gathered_plan(*args, capacity, expert_count)
    return slot_plan(*args)


def solution(mesh):
    return jax.shard_map(
        on_device,
        mesh=mesh,
        in_specs=(
            P(("expert", "replica"), None),
            P(("expert", "replica"), None),
            P(("expert", "replica"), None),
            P("expert", None, "replica"),
            P("expert", None, "replica"),
            P("expert", "replica", None),
        ),
        out_specs=P(("expert", "replica"), None),
        check_vma=False,
    )
```

time: 135 us -> 102 us (0.76); the launches traced: 133 us -> 102 us
  Pallas kernels: 129 us -> 100 us
  other arithmetic: 2.18 us -> 0 us
    pallas_call x1, Pallas kernels: 129 us -> 100 us  [gathered_plan(): pl.pallas_call(functools.partial(fused, depth, expert_count, capacity, *C...]
where the time goes in v1:
time: 102 us
  Pallas kernels  100 us (98%)
  local copies, waits for them, and re-layouts  1.76 us (2%)
    pallas_call x1, Pallas kernels, gathered_plan(): pl.pallas_call(functools.partial(fused, depth, expert_count, capacity, *C...  100 us

profile of v1, /device:TPU:0, one launch (start us, length us, event | category | flops | bytes accessed | tf_op | source)
XLA Modules:
  0.0 101.9 jit_solution(13864941612708332418)
XLA Ops:
  0.0 100.1 %shard_map.64 = bf16[64,2880]{1,0:T(8,128)(2,1)} custom-call(bf16[64,2880]{1,0:T(8,128)(2,1)} %tokens.1, s32[4,64]{1,0:T(4,128)} %bitcast.6, s32[4,64]{1,0:T(4,128)} %bitcast.7, bf16[1,720,2880]{2,1,0:T(8,128)(2,1)} %bitcast.4, bf16[1,720,2880]{2,1,0:T(8,128)(2,1)} %bitcast.5, bf16[1,720,2880]{2,1,0:T(8,128)(2,1)} %w_down.1), custom_call_target="tpu_custom_call" | custom-call | tf_op jit(solution)/shard_map/pallas_call | solution.py:414
  100.1 1.8 %copy.8 = bf16[64,2880]{1,0:T(8,128)(2,1)} copy(bf16[64,2880]{1,0:T(8,128)(2,1)} %shard_map.64) | data formatting | bytes 737280

commit v2 on v1

v2 whole, which is shorter than its diff:
```python
import functools

import jax
import jax.numpy as jnp
from jax import lax
from jax.experimental import pallas as pl
from jax.experimental.pallas import tpu as pltpu
from jax.sharding import PartitionSpec as P

MESH = pl.DeviceIdType.MESH
CORES = 2


def activate(gate, up):
    return gate * jax.nn.sigmoid(1.702 * gate) * (up + 1.0)


def spans(extent, step):
    return [(low, min(low + step, extent)) for low in range(0, extent, step)]


def fused(
    depth, experts, cap, in_parts, out_parts, plan,
    tokens, ids, codes, w_gate, w_up, w_down, out,
    tok, far_tok, meta, far_meta, y_pick, x_buf, wg, wu, wd, hid, part, c_in,
    x_out, x_in, y_out, y_in, z_out, z_in, mid_in, acc, far_acc, last_out, last_in,
    w_sem, m_s, m_r, fm_s, fm_r, fx_s,
    zt_s, zt_r, zf_s, zf_r, raw_s, raw_r, yp_s, yp_r, xa_s, xa_r, xb_s, xb_r, cc_s, cc_r,
    pc_s, pc_r, px_s, px_r, py_s, py_r, pz_s, pz_r, mi_r, last_s, last_r,
):
    rows, width = tokens.shape
    f32, bf16 = jnp.float32, jnp.bfloat16
    expert, replica = lax.axis_index("expert"), lax.axis_index("replica")
    z, y = expert // 2, expert % 2
    other = z * 2 + (1 - y)
    y_peer = {"expert": other}
    x_peer = {"replica": (replica + CORES) % (2 * CORES)}
    c_peer = {"replica": replica // CORES * CORES + (1 - replica % CORES)}
    group = 2 * cap
    own_slots, mine = pl.ds(0, cap), pl.ds(0, 2 * group)

    def z_peer(level):
        return {"expert": level * 2 + y}

    def ahead(step):
        return (z + step) % depth

    def send(src, dst, ssem, rsem, peer):
        pltpu.make_async_remote_copy(
            src_ref=src, dst_ref=dst, send_sem=ssem, recv_sem=rsem,
            device_id=peer, device_id_type=MESH,
        ).start()

    def arrived(dst, sem):
        pltpu.make_async_copy(dst, dst, sem).wait()

    def block_at(i):
        pairs = jnp.minimum(z, depth - 1 - z)
        inward = jnp.where(2 * z < depth, 1, -1)
        beside = jnp.where(i % 2 == 1, z + inward * ((i + 1) // 2), z - inward * (i // 2))
        beyond = jnp.where(2 * z < depth, i, depth - 1 - i)
        return jnp.where(i <= 2 * pairs, beside, beyond)

    def cols(parts, p):
        _, low, high = parts[p]
        return pl.ds(low, high - low)

    barrier = pltpu.get_barrier_semaphore()
    greeted = [y_peer, x_peer, c_peer] + [z_peer(ahead(step)) for step in range(1, depth)]
    for peer in greeted:
        pl.semaphore_signal(barrier, inc=1, device_id=peer, device_id_type=MESH)
    own_load = pltpu.make_async_copy(tokens, tok.at[z], w_sem.at[3])
    own_load.start()
    loads = [
        pltpu.make_async_copy(src.at[0], dst, w_sem.at[i])
        for i, (src, dst) in enumerate(((w_gate, wg), (w_up, wu), (w_down, wd)))
    ]
    for load in loads:
        load.start()

    label = lax.broadcasted_iota(jnp.int32, (experts, rows), 0)
    named = jnp.zeros((experts, rows), f32)
    weight = jnp.zeros((experts, rows), f32)
    for k in range(ids.shape[0]):
        same = label == ids[k : k + 1, :]
        named = named + jnp.where(same, 1.0, 0.0)
        weight = weight + jnp.where(same, codes[k : k + 1, :].astype(f32) / 65536.0, 0.0)
    upto = lax.broadcasted_iota(jnp.int32, (rows, rows), 0) <= lax.broadcasted_iota(
        jnp.int32, (rows, rows), 1
    )
    counts = jnp.dot(
        named.astype(bf16), jnp.where(upto, 1.0, 0.0).astype(bf16), preferred_element_type=f32
    )
    meta[z, pl.ds(0, experts), :] = jnp.where(named > 0, counts - 1.0, -1.0)
    meta[z, pl.ds(experts, experts), :] = weight

    pl.semaphore_wait(barrier, len(greeted))
    own_load.wait()

    def upward(s):
        return (s <= z) & (z < depth - 1)

    def downward(s):
        return (s >= z) & (z > 0)

    def pass_on(s, src, up_sem, down_sem, rsem):
        @pl.when(upward(s))
        def _():
            send(src, src, up_sem, rsem, z_peer(ahead(1)))

        @pl.when(downward(s))
        def _():
            send(src, src, down_sem, rsem, z_peer(ahead(depth - 1)))

    def passed(s, src, up_sem, down_sem):
        @pl.when(upward(s))
        def _():
            arrived(src, up_sem)

        @pl.when(downward(s))
        def _():
            arrived(src, down_sem)

    def pass_tok(p, s):
        pass_on(s, tok.at[s, :, cols(in_parts, p)], zt_s.at[p, 0, s], zt_s.at[p, 1, s], zt_r.at[p, s])

    def pass_far(p, s):
        pass_on(s, far_tok.at[s, :, cols(in_parts, p)], zf_s.at[p, 0, s], zf_s.at[p, 1, s], zf_r.at[p, s])

    def send_raw(p, s):
        c = cols(in_parts, p)
        send(tok.at[s, :, c], far_tok.at[s, :, c], raw_s.at[p, s], raw_r.at[p, s], x_peer)

    send(meta.at[z], far_meta.at[z], fx_s.at[0], fm_r.at[z], x_peer)
    pass_on(z, meta.at[z], m_s.at[0, z], m_s.at[1, z], m_r.at[z])
    for p in range(len(in_parts)):
        pass_tok(p, z)
    for p, (kind, _, _) in enumerate(in_parts):
        if kind != "A":
            send_raw(p, z)

    def row_of(table, which):
        sub = lax.broadcasted_iota(jnp.int32, table.shape, 0)
        return jnp.sum(jnp.where(sub == which, table, 0.0), axis=0, keepdims=True)

    def slots(table, which):
        slot = lax.broadcasted_iota(jnp.int32, (cap, rows), 0).astype(f32)
        return slot == row_of(table, which)

    def picker(table):
        return jnp.concatenate(
            [jnp.where(slots(table, e), 1.0, 0.0) for e in (expert, other)], axis=0
        ).astype(bf16)

    def spreader(table):
        high, low = [], []
        for e in (expert, other):
            share = row_of(table, e + experts)
            coarse = share.astype(bf16).astype(f32)
            here = slots(table, e)
            high.append(jnp.where(here, coarse, 0.0))
            low.append(jnp.where(here, share - coarse, 0.0))
        return jnp.concatenate(high + low, axis=0).astype(bf16)

    def spread(table, own, far):
        stacked = jnp.concatenate([own, far, own, far], axis=0)
        return lax.dot_general(
            spreader(table), stacked, (((0,), (0,)), ((), ())), preferred_element_type=f32
        )

    def greet(p, i):
        s = block_at(i)

        @pl.when(i > 0)
        def _():
            arrived(meta.at[s], m_r.at[s])
            pass_on(s, meta.at[s], m_s.at[0, s], m_s.at[1, s], m_r.at[s])

        arrived(far_meta.at[s], fm_r.at[s])
        pass_on(s, far_meta.at[s], fm_s.at[0, s], fm_s.at[1, s], fm_r.at[s])

    def relay(p, i):
        s = block_at(i)
        kind, c = in_parts[p][0], cols(in_parts, p)
        arrived(tok.at[s, :, c], zt_r.at[p, s])
        pass_tok(p, s)
        if kind == "C":
            arrived(far_tok.at[s, :, c], zf_r.at[p, s])
            pass_far(p, s)
        if kind == "B":
            send_raw(p, s)

    def choose(p, i):
        s = block_at(i)
        kind, c = in_parts[p][0], cols(in_parts, p)

        def pick(table, block, low):
            chosen = jnp.dot(picker(table[s]), block[s, :, c], preferred_element_type=f32).astype(bf16)
            x_buf[s, pl.ds(low, cap), c] = chosen[:cap]
            y_pick[s, pl.ds(low, cap), c] = chosen[cap:]

        if kind == "A":
            pick(meta, tok, 0)
            send(y_pick.at[s, own_slots, c], x_buf.at[s, pl.ds(group, cap), c],
                 yp_s.at[p, s], yp_r.at[p, s], y_peer)
            send(x_buf.at[s, own_slots, c], x_buf.at[s, pl.ds(cap, cap), c],
                 xa_s.at[p, s], xa_r.at[p, s], x_peer)
            return

        @pl.when((i == 0) | (kind == "B"))
        def _():
            arrived(far_tok.at[s, :, c], raw_r.at[p, s])
            if kind == "C":
                pass_far(p, s)

        pick(meta, tok, 0)
        pick(far_meta, far_tok, cap)
        send(y_pick.at[s, :, c], x_buf.at[s, pl.ds(group, group), c],
             yp_s.at[p, s], yp_r.at[p, s], y_peer)

    def forward(p, i):
        s = block_at(i)
        c = cols(in_parts, p)
        here = x_buf.at[s, pl.ds(group, cap), c]
        arrived(here, yp_r.at[p, s])
        send(here, x_buf.at[s, pl.ds(group + cap, cap), c], xb_s.at[p, s], xb_r.at[p, s], x_peer)

    def to_core(p, i):
        s = block_at(i)
        kind, c = in_parts[p][0], cols(in_parts, p)
        if kind == "A":
            arrived(x_buf.at[s, pl.ds(cap, cap), c], xa_r.at[p, s])
            arrived(x_buf.at[s, pl.ds(group + cap, cap), c], xb_r.at[p, s])
        else:
            arrived(x_buf.at[s, pl.ds(group, group), c], yp_r.at[p, s])
        send(x_buf.at[s, mine, c], x_buf.at[s, pl.ds(2 * group, 2 * group), c],
             cc_s.at[p, s], cc_r.at[p, s], c_peer)

    starts = dict(plan)
    first_up = min((t, i) for i, t in enumerate(starts["up", 0]))[1]
    thirds = spans(wg.shape[0], -(-wg.shape[0] // (3 * 128)) * 128)

    def up(p, i):
        s = block_at(i)
        if p == 0:
            for q in range(len(in_parts)):
                arrived(x_buf.at[s, mine, cols(in_parts, q)], cc_r.at[q, s])

            @pl.when(i == first_up)
            def _():
                for load in loads:
                    load.wait()

        across = (((1,), (1,)), ((), ()))
        low, high = thirds[p]
        block = x_buf[s]
        gate = lax.dot_general(block, wg[low:high, :], across, preferred_element_type=f32)
        more = lax.dot_general(block, wu[low:high, :], across, preferred_element_type=f32)
        hid[:, low:high] = activate(gate, more).astype(bf16)

    def down(p, i):
        s = block_at(i)
        _, start, stop = out_parts[p]
        for low, high in spans(stop - start, 512):
            here = slice(start + low, start + high)
            part[s, :, here] = jnp.dot(
                hid[...], wd[:, here], preferred_element_type=f32
            ).astype(bf16)
        c = cols(out_parts, p)
        send(part.at[s, pl.ds(2 * group, 2 * group), c], c_in.at[s, :, c],
             pc_s.at[p, s], pc_r.at[p, s], c_peer)

    def pair(s, low, count, c):
        return part[s, pl.ds(low, count), c].astype(f32) + c_in[s, pl.ds(low, count), c].astype(f32)

    def core(p, j):
        s = block_at(j)
        kind, c = out_parts[p][0], cols(out_parts, p)
        arrived(c_in.at[s, :, c], pc_r.at[p, s])
        if kind == "A":
            for n in range(2):
                x_out[s, pl.ds(n * cap, cap), c] = pair(s, cap + n * group, cap, c).astype(bf16)
            send(x_out.at[s, :, c], x_in.at[s, :, c], px_s.at[p, s], px_r.at[p, s], x_peer)
        else:
            y_out[s, :, c] = pair(s, group, group, c).astype(bf16)
            send(y_out.at[s, :, c], y_in.at[s, :, c], py_s.at[p, s], py_r.at[p, s], y_peer)

    def detour(source, owner):
        return ((source == 0) & (owner > 1)) | ((source == depth - 1) & (owner < depth - 2))

    def joins(s):
        return ((z == 1) & (s > 1)) | ((z == depth - 2) & (s < depth - 2))

    def z_rows(p):
        return pl.ds(0, 2 * rows if out_parts[p][0] == "C" else rows)

    def z_send(p, s, ready):
        c, r = cols(out_parts, p), z_rows(p)

        @pl.when(ready & detour(z, s))
        def _():
            send(z_out.at[s, r, c], mid_in.at[s, r, c], pz_s.at[p, s], mi_r.at[p, s],
                 z_peer(jnp.where(z == 0, 1, depth - 2)))

        @pl.when(ready & jnp.logical_not(detour(z, s)))
        def _():
            send(z_out.at[s, r, c], z_in.at[z, r, c], pz_s.at[p, s], pz_r.at[p, z], z_peer(s))

    def deliver(p, s, total, far=None):
        c = cols(out_parts, p)

        @pl.when(s == z)
        def _():
            acc[:, c] = total
            if far is not None:
                far_acc[:, c] = far

        @pl.when(s != z)
        def _():
            z_out[s, pl.ds(0, rows), c] = total.astype(bf16)
            if far is not None:
                z_out[s, pl.ds(rows, rows), c] = far.astype(bf16)

        z_send(p, s, (s != z) & jnp.logical_not(joins(s)))

    def far_mix(p, s):
        c = cols(out_parts, p)
        return spread(far_meta[s], pair(s, cap, cap, c).astype(bf16), y_in[s, pl.ds(cap, cap), c])

    def own_mix(p, s):
        c = cols(out_parts, p)
        return spread(meta[s], pair(s, 0, cap, c).astype(bf16), y_in[s, own_slots, c])

    def gather(p, j):
        s = block_at(j)
        kind, c = out_parts[p][0], cols(out_parts, p)
        if kind == "A":
            arrived(x_in.at[s, :, c], px_r.at[p, s])
            y_out[s, own_slots, c] = (
                pair(s, group, cap, c) + x_in[s, pl.ds(cap, cap), c].astype(f32)
            ).astype(bf16)
            send(y_out.at[s, own_slots, c], y_in.at[s, own_slots, c],
                 py_s.at[p, s], py_r.at[p, s], y_peer)
            return
        arrived(y_in.at[s, :, c], py_r.at[p, s])
        if kind == "B":
            x_out[s, pl.ds(0, rows), c] = far_mix(p, s).astype(bf16)
            send(x_out.at[s, pl.ds(0, rows), c], x_in.at[s, pl.ds(0, rows), c],
                 px_s.at[p, s], px_r.at[p, s], x_peer)
        else:
            deliver(p, s, own_mix(p, s), far_mix(p, s))

    def comb(p, j):
        s = block_at(j)
        kind, c = out_parts[p][0], cols(out_parts, p)
        if kind == "A":
            arrived(y_in.at[s, own_slots, c], py_r.at[p, s])
            own = (pair(s, 0, cap, c) + x_in[s, own_slots, c].astype(f32)).astype(bf16)
            deliver(p, s, spread(meta[s], own, y_in[s, own_slots, c]))
        else:
            arrived(x_in.at[s, pl.ds(0, rows), c], px_r.at[p, s])
            deliver(p, s, own_mix(p, s) + x_in[s, pl.ds(0, rows), c].astype(f32))

    def chain(p, j):
        s = block_at(j)
        c, r = cols(out_parts, p), z_rows(p)

        @pl.when(joins(s))
        def _():
            arrived(mid_in.at[s, r, c], mi_r.at[p, s])
            z_out[s, r, c] = (z_out[s, r, c].astype(f32) + mid_in[s, r, c].astype(f32)).astype(bf16)

        z_send(p, s, joins(s))

    table = {
        "meta": greet, "relay": relay, "choose": choose, "forward": forward, "to_core": to_core,
        "up": up, "down": down, "core": core, "sum": gather, "comb": comb, "chain": chain,
    }

    order = sorted((t, k, key, i) for k, (key, at) in enumerate(plan) for i, t in enumerate(at) if t is not None)
    for _, _, (name, p), i in order:
        table[name](p, i)

    def collect(p):
        kind, c = out_parts[p][0], cols(out_parts, p)
        for step in range(1, depth):
            q = ahead(step)

            @pl.when(jnp.logical_not(detour(q, z)))
            def _():
                arrived(z_in.at[q, z_rows(p), c], pz_r.at[p, q])
                acc[:, c] = acc[:, c] + z_in[q, pl.ds(0, rows), c].astype(f32)
                if kind == "C":
                    far_acc[:, c] = far_acc[:, c] + z_in[q, pl.ds(rows, rows), c].astype(f32)

    crossing = [p for p, (kind, _, _) in enumerate(out_parts) if kind == "C"]
    for p in crossing:
        c = cols(out_parts, p)
        collect(p)
        last_out[:, c] = far_acc[:, c].astype(bf16)
        send(last_out.at[:, c], last_in.at[:, c], last_s.at[p], last_r.at[p], x_peer)
    for p in range(len(out_parts)):
        if p not in crossing:
            c = cols(out_parts, p)
            collect(p)
            out[:, c] = acc[:, c].astype(bf16)
    for p in crossing:
        c = cols(out_parts, p)
        arrived(last_in.at[:, c], last_r.at[p])
        out[:, c] = (acc[:, c] + last_in[:, c].astype(f32)).astype(bf16)

    arrived(meta.at[0], fx_s.at[0])
    for p in crossing:
        arrived(last_out.at[:, cols(out_parts, p)], last_s.at[p])

    def settle(s, carry):
        passed(s, meta.at[s], m_s.at[0, s], m_s.at[1, s])
        passed(s, far_meta.at[s], fm_s.at[0, s], fm_s.at[1, s])
        for p, (kind, _, _) in enumerate(in_parts):
            c = cols(in_parts, p)
            passed(s, tok.at[s, :, c], zt_s.at[p, 0, s], zt_s.at[p, 1, s])
            if kind == "C":
                passed(s, far_tok.at[s, :, c], zf_s.at[p, 0, s], zf_s.at[p, 1, s])
            if kind != "A":
                @pl.when((s == z) | (kind == "B"))
                def _():
                    arrived(far_tok.at[s, :, c], raw_s.at[p, s])

                arrived(y_pick.at[s, :, c], yp_s.at[p, s])
            else:
                slab = x_buf.at[s, own_slots, c]
                for sem in (yp_s, xa_s, xb_s):
                    arrived(slab, sem.at[p, s])
            arrived(x_buf.at[s, mine, c], cc_s.at[p, s])
        for p, (kind, _, _) in enumerate(out_parts):
            c = cols(out_parts, p)
            arrived(c_in.at[s, :, c], pc_s.at[p, s])
            if kind == "A":
                arrived(x_out.at[s, :, c], px_s.at[p, s])
                arrived(y_out.at[s, own_slots, c], py_s.at[p, s])
            else:
                arrived(y_out.at[s, :, c], py_s.at[p, s])
                if kind == "B":
                    arrived(x_out.at[s, pl.ds(0, rows), c], px_s.at[p, s])

            @pl.when(s != z)
            def _():
                arrived(z_out.at[s, z_rows(p), c], pz_s.at[p, s])
        return carry

    lax.fori_loop(0, depth, settle, 0)


IN_PARTS = (("A", 0), ("A", 1024), ("C", 2048))
OUT_PARTS = (("A", 0), ("A", 1152), ("C", 1792), ("C", 2304))
PLAN = (
    (("sum", 1), (28, 33, 27, 26)),
    (("meta", 0), (0, 1, 2, 10)),
    (("relay", 0), (None, 2, 5, 9)),
    (("to_core", 0), (2, 8, 14, 18)),
    (("core", 2), (17, 16, 19, 23)),
    (("comb", 0), (33, 32, 29, 31)),
    (("relay", 1), (None, 1, 5, 11)),
    (("choose", 0), (0, 2, 6, 10)),
    (("choose", 1), (0, 1, 5, 13)),
    (("down", 3), (7, 13, 18, 22)),
    (("forward", 0), (0, 4, 11, 16)),
    (("core", 1), (11, 27, 19, 25)),
    (("chain", 0), (None, 32, 34, 33)),
    (("up", 2), (6, 12, 17, 21)),
    (("core", 0), (26, 17, 20, 25)),
    (("to_core", 1), (2, 7, 13, 17)),
    (("sum", 2), (24, 19, 21, 25)),
    (("chain", 2), (None, 25, 34, 29)),
    (("sum", 0), (31, 30, 25, 29)),
    (("choose", 2), (0, 3, 7, 14)),
    (("down", 2), (6, 14, 17, 21)),
    (("comb", 1), (30, 33, 31, 28)),
    (("core", 3), (10, 14, 20, 24)),
    (("up", 0), (3, 10, 16, 19)),
    (("chain", 3), (None, 27, 24, 30)),
    (("down", 0), (9, 14, 18, 21)),
    (("up", 1), (3, 11, 16, 19)),
    (("to_core", 2), (1, 6, 12, 16)),
    (("down", 1), (8, 15, 17, 23)),
    (("relay", 2), (None, 2, 6, 13)),
    (("sum", 3), (30, 17, 23, 25)),
    (("forward", 1), (0, 2, 8, 14)),
    (("chain", 1), (None, 34, 33, 30)),
)


def gathered_plan(tokens, expert_ids, gate_codes, w_gate, w_up, w_down, capacity, expert_count):
    rows, top = expert_ids.shape
    width = tokens.shape[1]
    w_gate, w_up = jnp.swapaxes(w_gate, 1, 2), jnp.swapaxes(w_up, 1, 2)
    part_width = w_gate.shape[1]
    depth = lax.axis_size("expert") // 2
    f32, bf16 = jnp.float32, jnp.bfloat16
    group = 2 * capacity
    vm, dma = pltpu.VMEM, pltpu.SemaphoreType.DMA

    def bounds(parts):
        lows = [low for _, low in parts]
        return [(kind, low, high) for (kind, low), high in zip(parts, lows[1:] + [width])]

    in_parts, out_parts = bounds(IN_PARTS), bounds(OUT_PARTS)
    ins, outs = len(in_parts), len(out_parts)
    two, one = dma((ins, 2, depth)), dma((ins, depth))
    block = vm((depth, group, width), bf16)
    pair = vm((depth, 2 * rows, width), bf16)
    return pl.pallas_call(
        functools.partial(fused, depth, expert_count, capacity, in_parts, out_parts, PLAN),
        out_shape=jax.ShapeDtypeStruct((rows, width), bf16),
        in_specs=[pl.BlockSpec(memory_space=pl.ANY)]
        + [pl.BlockSpec(memory_space=pltpu.VMEM)] * 2
        + [pl.BlockSpec(memory_space=pl.ANY)] * 3,
        out_specs=pl.BlockSpec(memory_space=pltpu.VMEM),
        scratch_shapes=[
            vm((depth, rows, width), bf16),
            vm((depth, rows, width), bf16),
            vm((depth, 2 * expert_count, rows), f32),
            vm((depth, 2 * expert_count, rows), f32),
            block,
            vm((depth, 4 * group, width), bf16),
            vm(w_gate.shape[1:], bf16),
            vm(w_up.shape[1:], bf16),
            vm(w_down.shape[1:], bf16),
            vm((4 * group, part_width), bf16),
            vm((depth, 4 * group, width), bf16),
            vm((depth, 2 * group, width), bf16),
            block,
            block,
            block,
            block,
            pair,
            pair,
            pair,
            vm((rows, width), f32),
            vm((rows, width), f32),
            vm((rows, width), bf16),
            vm((rows, width), bf16),
            dma((4,)),
            dma((2, depth)),
            dma((depth,)),
            dma((2, depth)),
            dma((depth,)),
            dma((1,)),
            two,
            one,
            two,
        ]
        + [one] * 11
        + [dma((outs, depth))] * 9
        + [dma((outs,))] * 2,
        compiler_params=pltpu.CompilerParams(
            collective_id=0, has_side_effects=True, vmem_limit_bytes=63 << 20
        ),
    )(tokens, expert_ids.T, gate_codes.T, w_gate, w_up, w_down)


def slot_plan(tokens, expert_ids, gate_codes, w_gate, w_up, w_down):
    tok_rows, top_count = expert_ids.shape
    width = tokens.shape[1]
    expert_count = lax.axis_size("expert") * w_gate.shape[0]
    capacity = 3 * tok_rows * top_count // (2 * expert_count)
    slot_count = expert_count * capacity
    flat_ids = expert_ids.reshape(-1)
    onehot = (flat_ids[:, None] == jnp.arange(expert_count, dtype=jnp.int32)[None, :]).astype(
        jnp.int32
    )
    ranking = jnp.sum((jnp.cumsum(onehot, axis=0) - 1) * onehot, axis=1)
    target = flat_ids * capacity + ranking
    picker = (target[:, None] == jnp.arange(slot_count, dtype=jnp.int32)[None, :]).astype(
        jnp.bfloat16
    )
    selector = jnp.sum(picker.reshape(tok_rows, top_count, slot_count), axis=1)
    outgoing = jnp.einsum("ts,td->sd", selector, tokens, preferred_element_type=jnp.float32).astype(
        jnp.bfloat16
    )
    arrived = lax.all_to_all(outgoing, "expert", split_axis=0, concat_axis=0, tiled=True)
    gathered = lax.all_gather(arrived, "replica", axis=0, tiled=True)
    gate = jnp.dot(gathered, w_gate[0], preferred_element_type=jnp.float32)
    up = jnp.dot(gathered, w_up[0], preferred_element_type=jnp.float32)
    hidden = activate(gate, up).astype(jnp.bfloat16)
    summed = lax.psum_scatter(
        jnp.dot(hidden, w_down[0], preferred_element_type=jnp.float32).astype(jnp.bfloat16),
        "replica",
        scatter_dimension=0,
        tiled=True,
    )
    returned = lax.all_to_all(summed, "expert", split_axis=0, concat_axis=0, tiled=True)
    per_choice = jnp.dot(picker, returned, preferred_element_type=jnp.float32)
    gates = gate_codes.astype(jnp.float32) / 65536.0
    weighted = per_choice.reshape(tok_rows, top_count, width) * gates[:, :, None]
    return jnp.sum(weighted, axis=1).astype(jnp.bfloat16)


def on_device(tokens, expert_ids, gate_codes, w_gate, w_up, w_down):
    rows, top = expert_ids.shape
    expert_count = lax.axis_size("expert") * w_gate.shape[0]
    capacity = 3 * rows * top // (2 * expert_count)
    args = (tokens, expert_ids, gate_codes, w_gate, w_up, w_down)
    paired = w_gate.shape[0] == 1 and lax.axis_size("replica") == 2 * CORES
    if paired and 2 * capacity > rows:
        return gathered_plan(*args, capacity, expert_count)
    return slot_plan(*args)


def solution(mesh):
    return jax.shard_map(
        on_device,
        mesh=mesh,
        in_specs=(
            P(("expert", "replica"), None),
            P(("expert", "replica"), None),
            P(("expert", "replica"), None),
            P("expert", None, "replica"),
            P("expert", None, "replica"),
            P("expert", "replica", None),
        ),
        out_specs=P(("expert", "replica"), None),
        check_vma=False,
    )
```

time: 102 us -> 95.2 us (0.933)
  Pallas kernels: 100 us -> 93.2 us
    pallas_call x1, Pallas kernels: 100 us -> 93.2 us  [gathered_plan(): pl.pallas_call(functools.partial(fused, depth, expert_count, capacity, in...]
where the time goes in v2:
time: 95.2 us; the launch traced here: 95 us
  Pallas kernels  93.2 us (98%)
  local copies, waits for them, and re-layouts  1.76 us (2%)
    pallas_call x1, Pallas kernels, gathered_plan(): pl.pallas_call(functools.partial(fused, depth, expert_count, capacity, in...  93.2 us

profile of v2, /device:TPU:0, one launch (start us, length us, event | category | flops | bytes accessed | tf_op | source)
XLA Modules:
  0.0 95.0 jit_solution(3731782476229811672)
XLA Ops:
  0.0 93.2 %shard_map.64 = bf16[64,2880]{1,0:T(8,128)(2,1)} custom-call(bf16[64,2880]{1,0:T(8,128)(2,1)} %tokens.1, s32[4,64]{1,0:T(4,128)} %bitcast.6, s32[4,64]{1,0:T(4,128)} %bitcast.7, bf16[1,720,2880]{2,1,0:T(8,128)(2,1)} %bitcast.4, bf16[1,720,2880]{2,1,0:T(8,128)(2,1)} %bitcast.5, bf16[1,720,2880]{2,1,0:T(8,128)(2,1)} %w_down.1), custom_call_target="tpu_custom_call" | custom-call | tf_op jit(solution)/shard_map/pallas_call | solution.py:512
  93.2 1.8 %copy.8 = bf16[64,2880]{1,0:T(8,128)(2,1)} copy(bf16[64,2880]{1,0:T(8,128)(2,1)} %shard_map.64) | data formatting | bytes 737280

commit v3 on v2

--- a/solution.py
+++ b/solution.py
@@ -21,10 +21,10 @@
 
 def fused(
     depth, experts, cap, in_parts, out_parts, plan,
-    tokens, ids, codes, w_gate, w_up, w_down, out,
-    tok, far_tok, meta, far_meta, y_pick, x_buf, wg, wu, wd, hid, part, c_in,
+    tokens, ids_in, codes_in, w_gate, w_up, w_down, out,
+    ids, codes, done, tok, far_tok, meta, far_meta, y_pick, x_buf, wg, wu, wd, hid, part, c_in,
     x_out, x_in, y_out, y_in, z_out, z_in, mid_in, acc, far_acc, last_out, last_in,
-    w_sem, m_s, m_r, fm_s, fm_r, fx_s,
+    w_sem, out_sem, m_s, m_r, fm_s, fm_r, fx_s,
     zt_s, zt_r, zf_s, zf_r, raw_s, raw_r, yp_s, yp_r, xa_s, xa_r, xb_s, xb_r, cc_s, cc_r,
     pc_s, pc_r, px_s, px_r, py_s, py_r, pz_s, pz_r, mi_r, last_s, last_r,
 ):
@@ -66,11 +66,21 @@
         return pl.ds(low, high - low)
 
     barrier = pltpu.get_barrier_semaphore()
-    greeted = [y_peer, x_peer, c_peer] + [z_peer(ahead(step)) for step in range(1, depth)]
-    for peer in greeted:
+    for peer in (y_peer, x_peer, c_peer):
         pl.semaphore_signal(barrier, inc=1, device_id=peer, device_id_type=MESH)
+    for inside, step in ((z < depth - 1, 1), (z > 0, depth - 1)):
+        @pl.when(inside)
+        def _():
+            pl.semaphore_signal(
+                barrier, inc=1, device_id=z_peer(ahead(step)), device_id_type=MESH
+            )
+
+    neighbours = 3 + jnp.where(z < depth - 1, 1, 0) + jnp.where(z > 0, 1, 0)
     own_load = pltpu.make_async_copy(tokens, tok.at[z], w_sem.at[3])
-    own_load.start()
+    id_load = pltpu.make_async_copy(ids_in, ids, w_sem.at[4])
+    code_load = pltpu.make_async_copy(codes_in, codes, w_sem.at[5])
+    for load in (own_load, id_load, code_load):
+        load.start()
     loads = [
         pltpu.make_async_copy(src.at[0], dst, w_sem.at[i])
         for i, (src, dst) in enumerate(((w_gate, wg), (w_up, wu), (w_down, wd)))
@@ -78,6 +88,46 @@
     for load in loads:
         load.start()
 
+    pl.semaphore_wait(barrier, neighbours)
+    own_load.wait()
+
+    def upward(s):
+        return (s <= z) & (z < depth - 1)
+
+    def downward(s):
+        return (s >= z) & (z > 0)
+
+    def pass_on(s, src, up_sem, down_sem, rsem):
+        @pl.when(upward(s))
+        def _():
+            send(src, src, up_sem, rsem, z_peer(ahead(1)))
+
+        @pl.when(downward(s))
+        def _():
+            send(src, src, down_sem, rsem, z_peer(ahead(depth - 1)))
+
+    def passed(s, src, up_sem, down_sem):
+        @pl.when(upward(s))
+        def _():
+            arrived(src, up_sem)
+
+        @pl.when(downward(s))
+        def _():
+            arrived(src, down_sem)
+
+    def pass_tok(p, s):
+        pass_on(s, tok.at[s, :, cols(in_parts, p)], zt_s.at[p, 0, s], zt_s.at[p, 1, s], zt_r.at[p, s])
+
+    def pass_far(p, s):
+        pass_on(s, far_tok.at[s, :, cols(in_parts, p)], zf_s.at[p, 0, s], zf_s.at[p, 1, s], zf_r.at[p, s])
+
+    def send_raw(p, s):
+        c = cols(in_parts, p)
+        send(tok.at[s, :, c], far_tok.at[s, :, c], raw_s.at[p, s], raw_r.at[p, s], x_peer)
+
+    pass_tok(0, z)
+    id_load.wait()
+    code_load.wait()
     label = lax.broadcasted_iota(jnp.int32, (experts, rows), 0)
     named = jnp.zeros((experts, rows), f32)
     weight = jnp.zeros((experts, rows), f32)
@@ -93,47 +143,9 @@
     )
     meta[z, pl.ds(0, experts), :] = jnp.where(named > 0, counts - 1.0, -1.0)
     meta[z, pl.ds(experts, experts), :] = weight
-
-    pl.semaphore_wait(barrier, len(greeted))
-    own_load.wait()
-
-    def upward(s):
-        return (s <= z) & (z < depth - 1)
-
-    def downward(s):
-        return (s >= z) & (z > 0)
-
-    def pass_on(s, src, up_sem, down_sem, rsem):
-        @pl.when(upward(s))
-        def _():
-            send(src, src, up_sem, rsem, z_peer(ahead(1)))
-
-        @pl.when(downward(s))
-        def _():
-            send(src, src, down_sem, rsem, z_peer(ahead(depth - 1)))
-
-    def passed(s, src, up_sem, down_sem):
-        @pl.when(upward(s))
-        def _():
-            arrived(src, up_sem)
-
-        @pl.when(downward(s))
-        def _():
-            arrived(src, down_sem)
-
-    def pass_tok(p, s):
-        pass_on(s, tok.at[s, :, cols(in_parts, p)], zt_s.at[p, 0, s], zt_s.at[p, 1, s], zt_r.at[p, s])
-
-    def pass_far(p, s):
-        pass_on(s, far_tok.at[s, :, cols(in_parts, p)], zf_s.at[p, 0, s], zf_s.at[p, 1, s], zf_r.at[p, s])
-
-    def send_raw(p, s):
-        c = cols(in_parts, p)
-        send(tok.at[s, :, c], far_tok.at[s, :, c], raw_s.at[p, s], raw_r.at[p, s], x_peer)
-
     send(meta.at[z], far_meta.at[z], fx_s.at[0], fm_r.at[z], x_peer)
     pass_on(z, meta.at[z], m_s.at[0, z], m_s.at[1, z], m_r.at[z])
-    for p in range(len(in_parts)):
+    for p in range(1, len(in_parts)):
         pass_tok(p, z)
     for p, (kind, _, _) in enumerate(in_parts):
         if kind != "A":
@@ -236,9 +248,9 @@
         send(x_buf.at[s, mine, c], x_buf.at[s, pl.ds(2 * group, 2 * group), c],
              cc_s.at[p, s], cc_r.at[p, s], c_peer)
 
-    starts = dict(plan)
-    first_up = min((t, i) for i, t in enumerate(starts["up", 0]))[1]
-    thirds = spans(wg.shape[0], -(-wg.shape[0] // (3 * 128)) * 128)
+    first_up = next(i for name, _, i in plan if name == "up")
+    ups = sum(1 for name, _, i in plan if name == "up" and i == first_up)
+    pieces = spans(wg.shape[0], 256)
 
     def up(p, i):
         s = block_at(i)
@@ -252,11 +264,11 @@
                     load.wait()
 
         across = (((1,), (1,)), ((), ()))
-        low, high = thirds[p]
-        block = x_buf[s]
-        gate = lax.dot_general(block, wg[low:high, :], across, preferred_element_type=f32)
-        more = lax.dot_general(block, wu[low:high, :], across, preferred_element_type=f32)
-        hid[:, low:high] = activate(gate, more).astype(bf16)
+        for low, high in pieces if ups == 1 else pieces[p::ups]:
+            block = x_buf[s]
+            gate = lax.dot_general(block, wg[low:high, :], across, preferred_element_type=f32)
+            more = lax.dot_general(block, wu[low:high, :], across, preferred_element_type=f32)
+            hid[:, low:high] = activate(gate, more).astype(bf16)
 
     def down(p, i):
         s = block_at(i)
@@ -377,8 +389,7 @@
         "up": up, "down": down, "core": core, "sum": gather, "comb": comb, "chain": chain,
     }
 
-    order = sorted((t, k, key, i) for k, (key, at) in enumerate(plan) for i, t in enumerate(at) if t is not None)
-    for _, _, (name, p), i in order:
+    for name, p, i in plan:
         table[name](p, i)
 
     def collect(p):
@@ -392,6 +403,10 @@
                 acc[:, c] = acc[:, c] + z_in[q, pl.ds(0, rows), c].astype(f32)
                 if kind == "C":
                     far_acc[:, c] = far_acc[:, c] + z_in[q, pl.ds(rows, rows), c].astype(f32)
+
+    def leave(p):
+        c = cols(out_parts, p)
+        pltpu.make_async_copy(done.at[:, c], out.at[:, c], out_sem.at[p]).start()
 
     crossing = [p for p, (kind, _, _) in enumerate(out_parts) if kind == "C"]
     for p in crossing:
@@ -403,11 +418,13 @@
         if p not in crossing:
             c = cols(out_parts, p)
             collect(p)
-            out[:, c] = acc[:, c].astype(bf16)
+            done[:, c] = acc[:, c].astype(bf16)
+            leave(p)
     for p in crossing:
         c = cols(out_parts, p)
         arrived(last_in.at[:, c], last_r.at[p])
-        out[:, c] = (acc[:, c] + last_in[:, c].astype(f32)).astype(bf16)
+        done[:, c] = (acc[:, c] + last_in[:, c].astype(f32)).astype(bf16)
+        leave(p)
 
     arrived(meta.at[0], fx_s.at[0])
     for p in crossing:
@@ -449,44 +466,38 @@
         return carry
 
     lax.fori_loop(0, depth, settle, 0)
-
-
-IN_PARTS = (("A", 0), ("A", 1024), ("C", 2048))
-OUT_PARTS = (("A", 0), ("A", 1152), ("C", 1792), ("C", 2304))
+    for p in range(len(out_parts)):
+        arrived(done.at[:, cols(out_parts, p)], out_sem.at[p])
+
+
+IN_PARTS = (("A", 0), ("A", 1152), ("C", 2048))
+OUT_PARTS = (("A", 0), ("A", 896), ("C", 1920), ("C", 2432))
 PLAN = (
-    (("sum", 1), (28, 33, 27, 26)),
-    (("meta", 0), (0, 1, 2, 10)),
-    (("relay", 0), (None, 2, 5, 9)),
-    (("to_core", 0), (2, 8, 14, 18)),
-    (("core", 2), (17, 16, 19, 23)),
-    (("comb", 0), (33, 32, 29, 31)),
-    (("relay", 1), (None, 1, 5, 11)),
-    (("choose", 0), (0, 2, 6, 10)),
-    (("choose", 1), (0, 1, 5, 13)),
-    (("down", 3), (7, 13, 18, 22)),
-    (("forward", 0), (0, 4, 11, 16)),
-    (("core", 1), (11, 27, 19, 25)),
-    (("chain", 0), (None, 32, 34, 33)),
-    (("up", 2), (6, 12, 17, 21)),
-    (("core", 0), (26, 17, 20, 25)),
-    (("to_core", 1), (2, 7, 13, 17)),
-    (("sum", 2), (24, 19, 21, 25)),
-    (("chain", 2), (None, 25, 34, 29)),
-    (("sum", 0), (31, 30, 25, 29)),
-    (("choose", 2), (0, 3, 7, 14)),
-    (("down", 2), (6, 14, 17, 21)),
-    (("comb", 1), (30, 33, 31, 28)),
-    (("core", 3), (10, 14, 20, 24)),
-    (("up", 0), (3, 10, 16, 19)),
-    (("chain", 3), (None, 27, 24, 30)),
-    (("down", 0), (9, 14, 18, 21)),
-    (("up", 1), (3, 11, 16, 19)),
-    (("to_core", 2), (1, 6, 12, 16)),
-    (("down", 1), (8, 15, 17, 23)),
-    (("relay", 2), (None, 2, 6, 13)),
-    (("sum", 3), (30, 17, 23, 25)),
-    (("forward", 1), (0, 2, 8, 14)),
-    (("chain", 1), (None, 34, 33, 30)),
+    ("meta", 0, 0), ("choose", 0, 0), ("choose", 1, 0), ("forward", 0, 0), ("choose", 2, 0),
+    ("relay", 1, 1), ("forward", 1, 0), ("meta", 0, 1), ("choose", 1, 1), ("to_core", 0, 0),
+    ("to_core", 2, 0), ("relay", 0, 1), ("choose", 0, 1), ("relay", 2, 1), ("choose", 2, 1),
+    ("to_core", 1, 0), ("forward", 1, 1), ("up", 0, 0), ("relay", 1, 2), ("forward", 0, 1),
+    ("meta", 0, 2), ("up", 1, 0), ("relay", 0, 2), ("choose", 0, 2), ("up", 2, 0),
+    ("to_core", 1, 1), ("choose", 1, 2), ("down", 2, 0), ("down", 3, 0), ("to_core", 2, 1),
+    ("meta", 0, 3), ("relay", 2, 2), ("choose", 2, 2), ("to_core", 0, 1), ("down", 0, 0),
+    ("forward", 0, 2), ("relay", 1, 3), ("choose", 1, 3), ("down", 1, 0), ("up", 0, 1),
+    ("forward", 1, 2), ("relay", 0, 3), ("choose", 0, 3), ("up", 1, 1), ("up", 2, 1),
+    ("down", 3, 1), ("to_core", 2, 2), ("down", 0, 1), ("to_core", 0, 2), ("forward", 1, 3),
+    ("relay", 2, 3), ("forward", 0, 3), ("to_core", 1, 2), ("choose", 2, 3), ("down", 2, 1),
+    ("down", 1, 1), ("core", 0, 1), ("up", 0, 2), ("to_core", 1, 3), ("core", 2, 1),
+    ("core", 1, 0), ("up", 1, 2), ("up", 2, 2), ("core", 3, 1), ("down", 2, 2), ("down", 0, 2),
+    ("sum", 2, 1), ("core", 2, 2), ("to_core", 2, 3), ("core", 2, 0), ("sum", 0, 1),
+    ("to_core", 0, 3), ("down", 1, 2), ("core", 0, 2), ("down", 3, 2), ("sum", 3, 1),
+    ("up", 0, 3), ("sum", 2, 2), ("up", 1, 3), ("core", 1, 2), ("up", 2, 3), ("sum", 0, 2),
+    ("comb", 0, 1), ("down", 1, 3), ("core", 3, 2), ("down", 3, 3), ("down", 2, 3),
+    ("core", 1, 3), ("comb", 0, 2), ("core", 3, 3), ("chain", 2, 1), ("core", 2, 3),
+    ("down", 0, 3), ("sum", 3, 2), ("core", 0, 3), ("sum", 1, 2), ("sum", 3, 3), ("core", 1, 1),
+    ("core", 0, 0), ("chain", 0, 1), ("chain", 3, 2), ("sum", 1, 3), ("sum", 2, 3),
+    ("chain", 3, 1), ("sum", 0, 3), ("chain", 0, 2), ("chain", 3, 3), ("sum", 1, 0),
+    ("comb", 1, 3), ("core", 3, 0), ("comb", 0, 3), ("comb", 1, 2), ("chain", 1, 2),
+    ("chain", 2, 3), ("sum", 1, 1), ("chain", 1, 3), ("chain", 2, 2), ("sum", 0, 0),
+    ("sum", 3, 0), ("sum", 2, 0), ("chain", 0, 3), ("comb", 1, 0), ("comb", 1, 1),
+    ("chain", 1, 1), ("comb", 0, 0),
 )
 
 
@@ -512,11 +523,12 @@
     return pl.pallas_call(
         functools.partial(fused, depth, expert_count, capacity, in_parts, out_parts, PLAN),
         out_shape=jax.ShapeDtypeStruct((rows, width), bf16),
-        in_specs=[pl.BlockSpec(memory_space=pl.ANY)]
-        + [pl.BlockSpec(memory_space=pltpu.VMEM)] * 2
-        + [pl.BlockSpec(memory_space=pl.ANY)] * 3,
-        out_specs=pl.BlockSpec(memory_space=pltpu.VMEM),
+        in_specs=[pl.BlockSpec(memory_space=pl.ANY)] * 6,
+        out_specs=pl.BlockSpec(memory_space=pl.ANY),
         scratch_shapes=[
+            vm((top, rows), jnp.int32),
+            vm((top, rows), jnp.int32),
+            vm((rows, width), bf16),
             vm((depth, rows, width), bf16),
             vm((depth, rows, width), bf16),
             vm((depth, 2 * expert_count, rows), f32),
@@ -540,7 +552,8 @@
             vm((rows, width), f32),
             vm((rows, width), bf16),
             vm((rows, width), bf16),
-            dma((4,)),
+            dma((6,)),
+            dma((outs,)),
             dma((2, depth)),
             dma((depth,)),
             dma((2, depth)),

time: 95.2 us -> 92.6 us (0.973)
  Pallas kernels: 93.2 us -> 90.7 us
    pallas_call x1, Pallas kernels: 93.2 us -> 90.7 us  [gathered_plan(): pl.pallas_call(functools.partial(fused, depth, expert_count, capacity, in...]
where the time goes in v3:
time: 92.6 us; the launch traced here: 92.4 us
  Pallas kernels  90.7 us (98%)
  local copies, waits for them, and re-layouts  1.76 us (2%)
    pallas_call x1, Pallas kernels, gathered_plan(): pl.pallas_call(functools.partial(fused, depth, expert_count, capacity, in...  90.7 us

profile of v3, /device:TPU:0, one launch (start us, length us, event | category | flops | bytes accessed | tf_op | source)
XLA Modules:
  0.0 92.4 jit_solution(8353526223565561970)
XLA Ops:
  0.0 90.7 %shard_map.64 = bf16[64,2880]{1,0:T(8,128)(2,1)} custom-call(bf16[64,2880]{1,0:T(8,128)(2,1)} %tokens.1, s32[4,64]{1,0:T(4,128)} %bitcast.6, s32[4,64]{1,0:T(4,128)} %bitcast.7, bf16[1,720,2880]{2,1,0:T(8,128)(2,1)} %bitcast.4, bf16[1,720,2880]{2,1,0:T(8,128)(2,1)} %bitcast.5, bf16[1,720,2880]{2,1,0:T(8,128)(2,1)} %w_down.1), custom_call_target="tpu_custom_call" | custom-call | tf_op jit(solution)/shard_map/pallas_call | solution.py:523
  90.7 1.8 %copy.8 = bf16[64,2880]{1,0:T(8,128)(2,1)} copy(bf16[64,2880]{1,0:T(8,128)(2,1)} %shard_map.64) | data formatting | bytes 737280

commit v4 on v3

--- a/solution.py
+++ b/solution.py
@@ -470,34 +470,33 @@
         arrived(done.at[:, cols(out_parts, p)], out_sem.at[p])
 
 
-IN_PARTS = (("A", 0), ("A", 1152), ("C", 2048))
+IN_PARTS = (("A", 0), ("A", 1024), ("C", 2176))
 OUT_PARTS = (("A", 0), ("A", 896), ("C", 1920), ("C", 2432))
 PLAN = (
-    ("meta", 0, 0), ("choose", 0, 0), ("choose", 1, 0), ("forward", 0, 0), ("choose", 2, 0),
-    ("relay", 1, 1), ("forward", 1, 0), ("meta", 0, 1), ("choose", 1, 1), ("to_core", 0, 0),
-    ("to_core", 2, 0), ("relay", 0, 1), ("choose", 0, 1), ("relay", 2, 1), ("choose", 2, 1),
-    ("to_core", 1, 0), ("forward", 1, 1), ("up", 0, 0), ("relay", 1, 2), ("forward", 0, 1),
-    ("meta", 0, 2), ("up", 1, 0), ("relay", 0, 2), ("choose", 0, 2), ("up", 2, 0),
-    ("to_core", 1, 1), ("choose", 1, 2), ("down", 2, 0), ("down", 3, 0), ("to_core", 2, 1),
-    ("meta", 0, 3), ("relay", 2, 2), ("choose", 2, 2), ("to_core", 0, 1), ("down", 0, 0),
-    ("forward", 0, 2), ("relay", 1, 3), ("choose", 1, 3), ("down", 1, 0), ("up", 0, 1),
-    ("forward", 1, 2), ("relay", 0, 3), ("choose", 0, 3), ("up", 1, 1), ("up", 2, 1),
-    ("down", 3, 1), ("to_core", 2, 2), ("down", 0, 1), ("to_core", 0, 2), ("forward", 1, 3),
-    ("relay", 2, 3), ("forward", 0, 3), ("to_core", 1, 2), ("choose", 2, 3), ("down", 2, 1),
-    ("down", 1, 1), ("core", 0, 1), ("up", 0, 2), ("to_core", 1, 3), ("core", 2, 1),
-    ("core", 1, 0), ("up", 1, 2), ("up", 2, 2), ("core", 3, 1), ("down", 2, 2), ("down", 0, 2),
-    ("sum", 2, 1), ("core", 2, 2), ("to_core", 2, 3), ("core", 2, 0), ("sum", 0, 1),
-    ("to_core", 0, 3), ("down", 1, 2), ("core", 0, 2), ("down", 3, 2), ("sum", 3, 1),
-    ("up", 0, 3), ("sum", 2, 2), ("up", 1, 3), ("core", 1, 2), ("up", 2, 3), ("sum", 0, 2),
-    ("comb", 0, 1), ("down", 1, 3), ("core", 3, 2), ("down", 3, 3), ("down", 2, 3),
-    ("core", 1, 3), ("comb", 0, 2), ("core", 3, 3), ("chain", 2, 1), ("core", 2, 3),
-    ("down", 0, 3), ("sum", 3, 2), ("core", 0, 3), ("sum", 1, 2), ("sum", 3, 3), ("core", 1, 1),
-    ("core", 0, 0), ("chain", 0, 1), ("chain", 3, 2), ("sum", 1, 3), ("sum", 2, 3),
-    ("chain", 3, 1), ("sum", 0, 3), ("chain", 0, 2), ("chain", 3, 3), ("sum", 1, 0),
-    ("comb", 1, 3), ("core", 3, 0), ("comb", 0, 3), ("comb", 1, 2), ("chain", 1, 2),
-    ("chain", 2, 3), ("sum", 1, 1), ("chain", 1, 3), ("chain", 2, 2), ("sum", 0, 0),
-    ("sum", 3, 0), ("sum", 2, 0), ("chain", 0, 3), ("comb", 1, 0), ("comb", 1, 1),
-    ("chain", 1, 1), ("comb", 0, 0),
+    ("meta", 0, 0), ("choose", 0, 0), ("choose", 1, 0), ("choose", 2, 0), ("forward", 0, 0),
+    ("relay", 0, 1), ("forward", 1, 0), ("meta", 0, 1), ("choose", 0, 1), ("relay", 1, 1),
+    ("to_core", 0, 0), ("to_core", 2, 0), ("relay", 2, 1), ("choose", 1, 1), ("to_core", 1, 0),
+    ("meta", 0, 2), ("choose", 2, 1), ("forward", 0, 1), ("relay", 0, 2), ("up", 0, 0),
+    ("forward", 1, 1), ("choose", 0, 2), ("up", 1, 0), ("up", 2, 0), ("to_core", 2, 1),
+    ("relay", 1, 2), ("choose", 1, 2), ("down", 2, 0), ("to_core", 0, 1), ("meta", 0, 3),
+    ("relay", 2, 2), ("choose", 2, 2), ("forward", 0, 2), ("relay", 0, 3), ("choose", 0, 3),
+    ("core", 2, 0), ("to_core", 1, 1), ("down", 0, 0), ("down", 1, 0), ("down", 3, 0),
+    ("forward", 1, 2), ("relay", 1, 3), ("choose", 1, 3), ("up", 0, 1), ("up", 1, 1),
+    ("to_core", 2, 2), ("up", 2, 1), ("to_core", 0, 2), ("down", 3, 1), ("forward", 0, 3),
+    ("relay", 2, 3), ("choose", 2, 3), ("to_core", 1, 2), ("down", 0, 1), ("forward", 1, 3),
+    ("down", 2, 1), ("core", 3, 1), ("core", 1, 0), ("down", 1, 1), ("up", 0, 2),
+    ("to_core", 0, 3), ("up", 1, 2), ("core", 2, 1), ("to_core", 1, 3), ("up", 2, 2),
+    ("to_core", 2, 3), ("core", 0, 1), ("down", 2, 2), ("down", 0, 2), ("sum", 3, 1),
+    ("down", 3, 2), ("sum", 2, 1), ("core", 2, 2), ("down", 1, 2), ("core", 0, 2), ("up", 0, 3),
+    ("up", 1, 3), ("core", 3, 2), ("sum", 0, 1), ("sum", 2, 2), ("core", 1, 2), ("up", 2, 3),
+    ("down", 3, 3), ("down", 1, 3), ("sum", 3, 2), ("core", 3, 3), ("down", 2, 3), ("core", 1, 3),
+    ("comb", 0, 1), ("chain", 2, 2), ("core", 2, 3), ("down", 0, 3), ("sum", 0, 2), ("sum", 3, 3),
+    ("chain", 3, 1), ("sum", 1, 2), ("core", 0, 3), ("core", 0, 0), ("chain", 2, 1),
+    ("sum", 2, 0), ("core", 1, 1), ("sum", 2, 3), ("sum", 1, 3), ("comb", 0, 2), ("chain", 3, 3),
+    ("sum", 0, 3), ("comb", 1, 3), ("core", 3, 0), ("chain", 3, 2), ("sum", 1, 0),
+    ("chain", 2, 3), ("comb", 0, 3), ("chain", 0, 2), ("chain", 0, 1), ("comb", 1, 2),
+    ("sum", 0, 0), ("sum", 3, 0), ("chain", 1, 3), ("sum", 1, 1), ("comb", 1, 0), ("chain", 0, 3),
+    ("comb", 0, 0), ("comb", 1, 1), ("chain", 1, 1), ("chain", 1, 2),
 )
 
 

time: 92.6 us -> 91.8 us (level)
  no operation moved by 1% of the time
where the time goes in v4:
time: 91.8 us; the launch traced here: 91.6 us
  Pallas kernels  89.9 us (98%)
  local copies, waits for them, and re-layouts  1.76 us (2%)
    pallas_call x1, Pallas kernels, gathered_plan(): pl.pallas_call(functools.partial(fused, depth, expert_count, capacity, in...  89.9 us

profile of v4, /device:TPU:0, one launch (start us, length us, event | category | flops | bytes accessed | tf_op | source)
XLA Modules:
  0.0 91.6 jit_solution(5150620271388159372)
XLA Ops:
  0.0 89.9 %shard_map.64 = bf16[64,2880]{1,0:T(8,128)(2,1)} custom-call(bf16[64,2880]{1,0:T(8,128)(2,1)} %tokens.1, s32[4,64]{1,0:T(4,128)} %bitcast.6, s32[4,64]{1,0:T(4,128)} %bitcast.7, bf16[1,720,2880]{2,1,0:T(8,128)(2,1)} %bitcast.4, bf16[1,720,2880]{2,1,0:T(8,128)(2,1)} %bitcast.5, bf16[1,720,2880]{2,1,0:T(8,128)(2,1)} %w_down.1), custom_call_target="tpu_custom_call" | custom-call | tf_op jit(solution)/shard_map/pallas_call | solution.py:522
  89.9 1.8 %copy.8 = bf16[64,2880]{1,0:T(8,128)(2,1)} copy(bf16[64,2880]{1,0:T(8,128)(2,1)} %shard_map.64) | data formatting | bytes 737280

commit v5 on v4

--- a/solution.py
+++ b/solution.py
@@ -392,6 +392,40 @@
     for name, p, i in plan:
         table[name](p, i)
 
+    def settle(s, carry):
+        passed(s, meta.at[s], m_s.at[0, s], m_s.at[1, s])
+        passed(s, far_meta.at[s], fm_s.at[0, s], fm_s.at[1, s])
+        for p, (kind, _, _) in enumerate(in_parts):
+            c = cols(in_parts, p)
+            passed(s, tok.at[s, :, c], zt_s.at[p, 0, s], zt_s.at[p, 1, s])
+            if kind == "C":
+                passed(s, far_tok.at[s, :, c], zf_s.at[p, 0, s], zf_s.at[p, 1, s])
+            if kind != "A":
+                @pl.when((s == z) | (kind == "B"))
+                def _():
+                    arrived(far_tok.at[s, :, c], raw_s.at[p, s])
+
+                arrived(y_pick.at[s, :, c], yp_s.at[p, s])
+            else:
+                slab = x_buf.at[s, own_slots, c]
+                for sem in (yp_s, xa_s, xb_s):
+                    arrived(slab, sem.at[p, s])
+            arrived(x_buf.at[s, mine, c], cc_s.at[p, s])
+        for p, (kind, _, _) in enumerate(out_parts):
+            c = cols(out_parts, p)
+            arrived(c_in.at[s, :, c], pc_s.at[p, s])
+            if kind == "A":
+                arrived(x_out.at[s, :, c], px_s.at[p, s])
+                arrived(y_out.at[s, own_slots, c], py_s.at[p, s])
+            else:
+                arrived(y_out.at[s, :, c], py_s.at[p, s])
+                if kind == "B":
+                    arrived(x_out.at[s, pl.ds(0, rows), c], px_s.at[p, s])
+        return carry
+
+    lax.fori_loop(0, depth, settle, 0)
+    arrived(meta.at[0], fx_s.at[0])
+
     def collect(p):
         kind, c = out_parts[p][0], cols(out_parts, p)
         for step in range(1, depth):
@@ -426,46 +460,13 @@
         done[:, c] = (acc[:, c] + last_in[:, c].astype(f32)).astype(bf16)
         leave(p)
 
-    arrived(meta.at[0], fx_s.at[0])
     for p in crossing:
         arrived(last_out.at[:, cols(out_parts, p)], last_s.at[p])
 
-    def settle(s, carry):
-        passed(s, meta.at[s], m_s.at[0, s], m_s.at[1, s])
-        passed(s, far_meta.at[s], fm_s.at[0, s], fm_s.at[1, s])
-        for p, (kind, _, _) in enumerate(in_parts):
-            c = cols(in_parts, p)
-            passed(s, tok.at[s, :, c], zt_s.at[p, 0, s], zt_s.at[p, 1, s])
-            if kind == "C":
-                passed(s, far_tok.at[s, :, c], zf_s.at[p, 0, s], zf_s.at[p, 1, s])
-            if kind != "A":
-                @pl.when((s == z) | (kind == "B"))
-                def _():
-                    arrived(far_tok.at[s, :, c], raw_s.at[p, s])
-
-                arrived(y_pick.at[s, :, c], yp_s.at[p, s])
-            else:
-                slab = x_buf.at[s, own_slots, c]
-                for sem in (yp_s, xa_s, xb_s):
-                    arrived(slab, sem.at[p, s])
-            arrived(x_buf.at[s, mine, c], cc_s.at[p, s])
-        for p, (kind, _, _) in enumerate(out_parts):
-            c = cols(out_parts, p)
-            arrived(c_in.at[s, :, c], pc_s.at[p, s])
-            if kind == "A":
-                arrived(x_out.at[s, :, c], px_s.at[p, s])
-                arrived(y_out.at[s, own_slots, c], py_s.at[p, s])
-            else:
-                arrived(y_out.at[s, :, c], py_s.at[p, s])
-                if kind == "B":
-                    arrived(x_out.at[s, pl.ds(0, rows), c], px_s.at[p, s])
-
-            @pl.when(s != z)
-            def _():
-                arrived(z_out.at[s, z_rows(p), c], pz_s.at[p, s])
-        return carry
-
-    lax.fori_loop(0, depth, settle, 0)
+    for step in range(1, depth):
+        s = ahead(step)
+        for p in range(len(out_parts)):
+            arrived(z_out.at[s, z_rows(p), cols(out_parts, p)], pz_s.at[p, s])
     for p in range(len(out_parts)):
         arrived(done.at[:, cols(out_parts, p)], out_sem.at[p])
 

time: 91.8 us -> 91.9 us (level)
  no operation moved by 1% of the time
where the time goes in v5:
time: 91.9 us; the launch traced here: 91.8 us
  Pallas kernels  90 us (98%)
  local copies, waits for them, and re-layouts  1.76 us (2%)
    pallas_call x1, Pallas kernels, gathered_plan(): pl.pallas_call(functools.partial(fused, depth, expert_count, capacity, in...  90 us

profile of v5, /device:TPU:0, one launch (start us, length us, event | category | flops | bytes accessed | tf_op | source)
XLA Modules:
  0.0 91.8 jit_solution(12458266500678369513)
XLA Ops:
  0.0 90.0 %shard_map.64 = bf16[64,2880]{1,0:T(8,128)(2,1)} custom-call(bf16[64,2880]{1,0:T(8,128)(2,1)} %tokens.1, s32[4,64]{1,0:T(4,128)} %bitcast.6, s32[4,64]{1,0:T(4,128)} %bitcast.7, bf16[1,720,2880]{2,1,0:T(8,128)(2,1)} %bitcast.4, bf16[1,720,2880]{2,1,0:T(8,128)(2,1)} %bitcast.5, bf16[1,720,2880]{2,1,0:T(8,128)(2,1)} %w_down.1), custom_call_target="tpu_custom_call" | custom-call | tf_op jit(solution)/shard_map/pallas_call | solution.py:523
  90.0 1.8 %copy.8 = bf16[64,2880]{1,0:T(8,128)(2,1)} copy(bf16[64,2880]{1,0:T(8,128)(2,1)} %shard_map.64) | data formatting | bytes 737280
